TPU v7x, 128 devices: a whole 4x4x4 slice. The times are simulated.
128 devices in a mesh: dp: 4 (over y_hi, core), mp: 32 (over x, z, y_lo).
Axes of the slice: x: 4, y: 4 (y_hi: 2, y_lo: 2; y = y_hi * 2 + y_lo), z: 4, core: 2. Of those that a mesh axis runs over, the one named last changes fastest.
Arguments:
- step_ids: int32 [32, 4], P('dp'), may hold values from 0 to 31999
- prompt_lens: int32 [32], P('dp'), may hold values from 128 to 1024
- embed_table: bfloat16 [32000, 4096], P(None, 'mp'), may hold values from -170 to 170
- attn_gain: bfloat16 [4096], replicated, may hold values from 0.099609375 to 1.8984375
- w_qkv: bfloat16 [3, 4096, 4096], P(None, None, 'mp'), may hold values from -0.09375 to 0.09375
- w_out: bfloat16 [4096, 4096], P('mp'), may hold values from -0.1875 to 0.1875
- key_cache: bfloat16 [32, 32, 1024, 128], P('dp', 'mp'), may hold values from -194 to 194
- value_cache: bfloat16 [32, 32, 1024, 128], P('dp', 'mp'), may hold values from -6 to 6
- reward_pieces: bfloat16 [32, 4096, 4096], P('dp', None, 'mp'), may hold values from -170 to 170
- piece_lens: int32 [32], P('dp'), may hold values from 256 to 4096
- reward_gain: bfloat16 [4096], replicated, may hold values from 0.099609375 to 1.8984375
- w_value: bfloat16 [4096, 2048], P('mp'), may hold values from -0.09375 to 0.09375
- b_value: float32 [2048], replicated, may hold values from -4 to 4
- w_score: float32 [2048], replicated, may hold values from -0.125 to 0.125
- b_score: float32 [1], replicated, may hold values from -3 to 3
Outputs:
- attn_out: bfloat16 [32, 4, 4096], P('dp')
- piece_values: float32 [32, 4096], P('dp', 'mp')
All inputs are finite; a program needn't handle non-finite values.
Results may differ from a plain program's by a relative error of at most 0.015.
Values may be sent and summed in bfloat16 or wider, within the bound.
No kernel may reach another device: no remote copies, remote signals or barrier semaphores. Data moves between devices by JAX's collectives and lax.ppermute only.
A program may use at most 192 MiB of HBM per device.

v0:
```python
import functools
import math

import jax
import jax.numpy as jnp
from jax import lax
from jax.experimental import pallas as pl
from jax.experimental.pallas import tpu as pltpu
from jax.sharding import Mesh, PartitionSpec as P


EPS = 1e-05
MASKED = -1e30
DP = ("yhi", "core")
MP = ("x", "z", "ylo")
GROUP = 32
LANES = 128
COLS = 512
HALF = 256
CHUNK = 4
RECEIVED = ((0, 0, 4), (-1, 0, 4), (1, 0, 4), (2, 0, 2), (2, 2, 4))


def vmem():
    return pl.BlockSpec(memory_space=pltpu.VMEM)


def hbm():
    return pl.BlockSpec(memory_space=pl.ANY)


def attention_kernel(row, message_ref, gain_ref, wqkv_hbm, cos_ref, sin_ref, lens_ref, key_hbm, value_hbm, wout_hbm, out_ref, *scratch):
    emb_ref, wqkv_ref, key_ref, value_ref, wout_ref, normed_ref, sems = scratch
    tokens = emb_ref.shape[1]
    copies = [
        pltpu.make_async_copy(source, target, sems.at[i])
        for i, (source, target) in enumerate(
            [
                (message_ref.at[:, pl.ds(row, tokens), :], emb_ref),
                (wqkv_hbm, wqkv_ref),
                (key_hbm, key_ref),
                (value_hbm, value_ref),
                (wout_hbm, wout_ref),
            ]
        )
    ]
    for copy in copies:
        copy.start()
    width = GROUP * LANES
    rows = key_ref.shape[0]
    steps = tokens // rows
    copies[0].wait()
    squares = jnp.zeros((tokens, LANES), jnp.float32)
    for s in range(GROUP):
        part = emb_ref[s].astype(jnp.float32)
        squares = squares + part * part
    mean = jnp.sum(squares, axis=-1, keepdims=True) / width
    inverse_rms = lax.rsqrt(mean + EPS)
    for s in range(GROUP):
        part = emb_ref[s].astype(jnp.float32) * inverse_rms * gain_ref[s : s + 1, :]
        normed_ref[:, s * LANES : (s + 1) * LANES] = part.astype(jnp.bfloat16)
    normed = normed_ref[...]
    copies[1].wait()
    parts = [jnp.dot(normed, wqkv_ref[c], preferred_element_type=jnp.float32) for c in range(3)]
    cos, sin = cos_ref[...], sin_ref[...]
    half = LANES // 2

    def rotate(v):
        return (v * cos + pltpu.roll(v, half, 1) * sin).astype(jnp.bfloat16)

    queries, new_keys = rotate(parts[0]), rotate(parts[1])
    new_values = parts[2].astype(jnp.bfloat16)
    root = 1.0 / math.sqrt(LANES)
    slots = key_ref.shape[1]
    group_of = lax.broadcasted_iota(jnp.int32, (tokens, slots), 0) // steps
    scores = jnp.zeros((tokens, slots), jnp.float32)
    copies[2].wait()
    for r in range(rows):
        one = lax.dot_general(queries, key_ref[r], (((1,), (1,)), ((), ())), preferred_element_type=jnp.float32)
        scores = jnp.where(group_of == r, one, scores)
    live = lax.broadcasted_iota(jnp.int32, (tokens, slots), 1) < lens_ref[:, 0:1]
    scores = jnp.where(live, scores * root, MASKED)
    fresh = lax.dot_general(queries, new_keys, (((1,), (1,)), ((), ())), preferred_element_type=jnp.float32)
    i = lax.broadcasted_iota(jnp.int32, (tokens, tokens), 0)
    j = lax.broadcasted_iota(jnp.int32, (tokens, tokens), 1)
    causal = (i // steps == j // steps) & (j <= i)
    fresh = jnp.where(causal, fresh * root, MASKED)
    top = jnp.maximum(jnp.max(scores, axis=-1, keepdims=True), jnp.max(fresh, axis=-1, keepdims=True))
    weights = jnp.exp(scores - top)
    fresh_weights = jnp.exp(fresh - top)
    total = jnp.sum(weights, axis=-1, keepdims=True) + jnp.sum(fresh_weights, axis=-1, keepdims=True)
    mixed = jnp.dot(fresh_weights.astype(jnp.bfloat16), new_values, preferred_element_type=jnp.float32)
    copies[3].wait()
    for r in range(rows):
        own = jnp.where(group_of == r, weights, 0.0).astype(jnp.bfloat16)
        mixed = mixed + jnp.dot(own, value_ref[r], preferred_element_type=jnp.float32)
    heads = (mixed / total).astype(jnp.bfloat16)
    copies[4].wait()
    partial = jnp.dot(heads, wout_ref[...], preferred_element_type=jnp.float32)
    high = partial.astype(jnp.bfloat16)
    out_ref[0:tokens, :] = high
    out_ref[tokens:, :] = (partial - high.astype(jnp.float32)).astype(jnp.bfloat16)


def attention(message, row, tokens, gain, w_qkv, cos, sin, lens, keys, values, w_out):
    loaded = [pltpu.VMEM(a.shape, a.dtype) for a in (w_qkv, keys, values, w_out)]
    return pl.pallas_call(
        functools.partial(attention_kernel, row),
        out_shape=jax.ShapeDtypeStruct((2 * tokens, GROUP * LANES), jnp.bfloat16),
        in_specs=[hbm(), vmem(), hbm(), vmem(), vmem(), vmem(), hbm(), hbm(), hbm()],
        out_specs=vmem(),
        scratch_shapes=[pltpu.VMEM((GROUP, tokens, LANES), jnp.bfloat16)]
        + loaded
        + [pltpu.VMEM((tokens, GROUP * LANES), jnp.bfloat16), pltpu.SemaphoreType.DMA((5,))],
        compiler_params=pltpu.CompilerParams(vmem_limit_bytes=62 << 20),
        cost_estimate=pl.CostEstimate(flops=4 * 10**8, bytes_accessed=9 << 20, transcendentals=40000),
        name="attention",
    )(message, gain, w_qkv, cos, sin, lens, keys, values, w_out)


def combine_kernel(first, base, message_ref, *refs):
    scored, (out_ref, buf, payload, sem) = refs[:-4], refs[-4:]
    tokens = buf.shape[1] // 2
    copy = pltpu.make_async_copy(message_ref.at[:, pl.ds(first, 2 * tokens), :], buf, sem.at[0])
    copy.start()
    payload[tokens:, :] = jnp.zeros((payload.shape[0] - tokens, LANES), jnp.float32)
    for i, part in enumerate(scored):
        at = tokens + i * base
        payload[at : at + part.shape[0], :] = part[...]
    copy.wait()
    total = jnp.zeros((tokens, LANES), jnp.float32)
    for s in range(GROUP):
        total = total + (buf[s, 0:tokens, :].astype(jnp.float32) + buf[s, tokens:, :].astype(jnp.float32))
    payload[0:tokens, :] = total.astype(jnp.bfloat16).astype(jnp.float32)
    for d in range(GROUP):
        pltpu.make_async_copy(payload, out_ref.at[d], sem.at[1]).start()
    pltpu.make_async_copy(out_ref, out_ref, sem.at[1]).wait()


def combine(message, first, base, tokens, scored):
    rows = tokens + 2 * base
    return pl.pallas_call(
        functools.partial(combine_kernel, first, base),
        out_shape=jax.ShapeDtypeStruct((GROUP, rows, LANES), jnp.float32),
        in_specs=[hbm()] + [vmem()] * len(scored),
        out_specs=pl.BlockSpec(memory_space=pltpu.HBM),
        scratch_shapes=[
            pltpu.VMEM((GROUP, 2 * tokens, LANES), jnp.bfloat16),
            pltpu.VMEM((rows, LANES), jnp.float32),
            pltpu.SemaphoreType.DMA((2,)),
        ],
        compiler_params=pltpu.CompilerParams(vmem_limit_bytes=62 << 20),
        cost_estimate=pl.CostEstimate(flops=10**5, bytes_accessed=1 << 19, transcendentals=0),
        name="combine",
    )(message, *scored)


def score_kernel(slots, place_ref, x_hbm, *refs):
    w_hbm, (gain_ref, bias_ref, score_ref, out_ref) = refs[:20], refs[20:24]
    x_buf, w_buf, normed_ref, total_ref, x_sem, w_sems = refs[24:]
    width = GROUP * LANES
    rows = slots * LANES
    x_copy = pltpu.make_async_copy(x_hbm.at[:, pl.ds(0, rows), :], x_buf, x_sem.at[0])
    x_copy.start()
    core, x, z, ylo = place_ref[0], place_ref[1], place_ref[2], place_ref[3]
    for side in range(2):
        owner = core if side == 0 else 1 - core
        near = jnp.where(owner == 0, z, x)
        far = jnp.where(owner == 0, x, z)
        for index, (step, begin, end) in enumerate(RECEIVED + RECEIVED):
            last = (far + step) & 3
            low = ylo if index < len(RECEIVED) else 1 - ylo

            @pl.loop(begin, end)
            def _(a):
                mine = (near + jnp.where(a < 2, -a, a - 1)) & 3
                block = jnp.where(owner == 0, last * 4 + mine, mine * 4 + last) * 2 + low
                pltpu.make_async_copy(
                    w_hbm[side * 10 + index].at[pl.ds(pl.multiple_of((a - begin) * LANES, LANES), LANES), :],
                    w_buf.at[owner, pl.ds(pl.multiple_of(block * LANES, LANES), LANES), :],
                    w_sems.at[owner],
                ).start()

    x_copy.wait()

    @pl.loop(0, slots)
    def _(q):
        here = pl.ds(pl.multiple_of(q * LANES, LANES), LANES)

        def square(c, squares):
            for i in range(CHUNK):
                part = x_buf[c * CHUNK + i, here, :].astype(jnp.float32)
                squares = squares + part * part
            return squares

        squares = lax.fori_loop(0, GROUP // CHUNK, square, jnp.zeros((LANES, LANES), jnp.float32))
        mean = jnp.sum(squares, axis=-1, keepdims=True) / width
        inverse_rms = lax.rsqrt(mean + EPS)

        @pl.loop(0, GROUP // CHUNK)
        def _(c):
            for i in range(CHUNK):
                s = c * CHUNK + i
                part = x_buf[s, here, :].astype(jnp.float32) * inverse_rms * gain_ref[pl.ds(s, 1), :]
                normed_ref[here, pl.ds(pl.multiple_of(s * LANES, LANES), LANES)] = part.astype(jnp.bfloat16)

    total_ref[...] = jnp.zeros_like(total_ref)

    @pl.loop(0, 4)
    def _(i):
        owner = jnp.where(i < 2, core, 1 - core)
        h = i & 1

        @pl.when(h == 0)
        def _():
            pltpu.make_async_copy(w_buf.at[owner], w_buf.at[owner], w_sems.at[owner]).wait()

        bias, score = bias_ref[pl.ds(owner * 2 + h, 1), :], score_ref[pl.ds(owner * 2 + h, 1), :]
        w = w_buf[owner, :, pl.ds(pl.multiple_of(h * COLS, COLS), COLS)]
        for part in range(0, rows, HALF):
            some = slice(part, min(part + HALF, rows))
            pre = jnp.dot(normed_ref[some, :], w, preferred_element_type=jnp.float32) + bias
            hidden = pre / (1.0 + jnp.exp(-pre)) * score
            total = total_ref[some, :]
            for c in range(COLS // LANES):
                total = total + hidden[:, c * LANES : (c + 1) * LANES]
            total_ref[some, :] = total

    for q in range(slots):
        out_ref[q : q + 1, :] = jnp.sum(total_ref[q * LANES : (q + 1) * LANES, :].T, axis=0, keepdims=True)


def score_rows(message, slots, place, parts, gain, bias, w_score):
    width = GROUP * LANES
    rows = slots * LANES
    return pl.pallas_call(
        functools.partial(score_kernel, slots),
        out_shape=jax.ShapeDtypeStruct((slots, LANES), jnp.float32),
        in_specs=[pl.BlockSpec(memory_space=pltpu.SMEM)] + [hbm()] * 21 + [vmem()] * 3,
        out_specs=vmem(),
        scratch_shapes=[
            pltpu.VMEM((GROUP, rows, LANES), jnp.bfloat16),
            pltpu.VMEM((2, width, 2 * COLS), jnp.bfloat16),
            pltpu.VMEM((rows, width), jnp.bfloat16),
            pltpu.VMEM((rows, LANES), jnp.float32),
            pltpu.SemaphoreType.DMA((1,)),
            pltpu.SemaphoreType.DMA((2,)),
        ],
        compiler_params=pltpu.CompilerParams(vmem_limit_bytes=62 << 20),
        cost_estimate=pl.CostEstimate(
            flops=2 * rows * width * 4 * COLS, bytes_accessed=24 << 20, transcendentals=rows * 4 * COLS
        ),
        name="score",
    )(place, message, *parts, gain, bias, w_score)


def block_starts(lens_ref, pieces):
    starts, counts = [], []
    start = 0
    for i in range(pieces):
        count = lax.shift_right_logical(lens_ref[i] + (LANES - 1), 7)
        starts.append(start)
        counts.append(count)
        start = start + count
    return starts, counts


def pack_kernel(pieces, first, slots, lens_ref, pieces_ref, *refs):
    starts, _ = block_starts(lens_ref, pieces)
    blocks = pieces_ref.shape[1] // LANES
    rows = slots * LANES
    if first:
        partial_ref, out_ref, stage, in_sems, out_sem = refs
        extra = partial_ref.shape[0]
    else:
        ids_ref, table_ref, out_ref, stage, tiles, picked, in_sems, out_sem = refs
        tokens = ids_ref.shape[0] * ids_ref.shape[1]
        steps = ids_ref.shape[1]
        for i in range(tokens):
            above = lax.shift_right_logical(ids_ref[i // steps, i % steps], 3) * 8
            pltpu.make_async_copy(table_ref.at[pl.ds(pl.multiple_of(above, 8), 8), :], tiles.at[i], in_sems.at[4]).start()
    chunk = GROUP // 4

    @pl.loop(0, GROUP)
    def _(d):
        sem = in_sems.at[d // chunk]

        @pl.loop(0, slots)
        def _(q):
            slot = (first + q) * GROUP + d
            piece, start = 0, 0
            for i in range(1, pieces):
                after = slot >= starts[i]
                piece = jnp.where(after, i, piece)
                start = jnp.where(after, starts[i], start)
            block = jnp.minimum(slot - start, blocks - 1)
            pltpu.make_async_copy(
                pieces_ref.at[piece, pl.ds(pl.multiple_of(block * LANES, LANES), LANES), :],
                stage.at[d, pl.ds(pl.multiple_of(q * LANES, LANES), LANES), :],
                sem,
            ).start()

        if first:
            source = partial_ref.at[:, pl.ds(pl.multiple_of(d * LANES, LANES), LANES)]
            pltpu.make_async_copy(source, stage.at[d, pl.ds(rows, extra), :], sem).start()

    if not first:
        pltpu.make_async_copy(tiles, tiles, in_sems.at[4]).wait()
        sublane = lax.broadcasted_iota(jnp.int32, (8, LANES), 0)
        for i in range(tokens):
            own = sublane == (ids_ref[i // steps, i % steps] & 7)
            picked[i : i + 1, :] = jnp.sum(jnp.where(own, tiles[i].astype(jnp.float32), 0.0), axis=0, keepdims=True)
        block = picked[...].astype(jnp.bfloat16)
        for d in range(GROUP):
            stage[d, rows:, :] = block
    done = stage.shape[1] if first else rows
    for c in range(4):
        part = pl.ds(c * chunk, chunk)
        landed = stage.at[part, pl.ds(0, done), :]
        pltpu.make_async_copy(landed, landed, in_sems.at[c]).wait()
        pltpu.make_async_copy(stage.at[part], out_ref.at[part], out_sem.at[c]).start()
    for c in range(4):
        part = pl.ds(c * chunk, chunk)
        pltpu.make_async_copy(stage.at[part], out_ref.at[part], out_sem.at[c]).wait()


def pack(first, slots, extra, scratch, operands, specs):
    rows = slots * LANES + extra
    return pl.pallas_call(
        functools.partial(pack_kernel, operands[1].shape[0], first, slots),
        out_shape=jax.ShapeDtypeStruct((GROUP, rows, LANES), jnp.bfloat16),
        in_specs=[pl.BlockSpec(memory_space=pltpu.SMEM), hbm()] + specs,
        out_specs=pl.BlockSpec(memory_space=pltpu.HBM),
        scratch_shapes=[pltpu.VMEM((GROUP, rows, LANES), jnp.bfloat16)]
        + scratch
        + [pltpu.SemaphoreType.DMA((5,)), pltpu.SemaphoreType.DMA((4,))],
        compiler_params=pltpu.CompilerParams(vmem_limit_bytes=62 << 20),
        cost_estimate=pl.CostEstimate(flops=0, bytes_accessed=4 * GROUP * rows * LANES, transcendentals=0),
    )(*operands)


def pack_first(slots, piece_lens, pieces, step_ids, embed_table):
    tokens = step_ids.shape[0] * step_ids.shape[1]
    scratch = [pltpu.VMEM((tokens, 8, LANES), jnp.bfloat16), pltpu.VMEM((tokens, LANES), jnp.float32)]
    specs = [pl.BlockSpec(memory_space=pltpu.SMEM), hbm()]
    return pack(0, slots, tokens, scratch, (piece_lens, pieces, step_ids, embed_table), specs)


def pack_rest(first, slots, piece_lens, pieces, partial):
    return pack(first, slots, partial.shape[0], [], (piece_lens, pieces, partial), [hbm()])


def finish_kernel(pieces, tokens, scalars_ref, offset_ref, result_ref, attn_ref, value_ref):
    starts, counts = block_starts(scalars_ref, pieces)
    me = scalars_ref[pieces]
    where = me * LANES + lax.broadcasted_iota(jnp.int32, (1, LANES), 1)
    for i in range(pieces):
        slot = jnp.minimum(starts[i] + jnp.minimum(me, counts[i]), pieces * GROUP - 1)
        row = result_ref[slot & (GROUP - 1), pl.ds(tokens + lax.shift_right_logical(slot, 5), 1), :]
        value_ref[i : i + 1, :] = jnp.where(where < scalars_ref[i], row + offset_ref[0], 0.0)
    rows, steps, _ = attn_ref.shape
    for s in range(GROUP):
        block = result_ref[s, 0:tokens, :].reshape(rows, steps, LANES)
        attn_ref[:, :, s * LANES : (s + 1) * LANES] = block.astype(jnp.bfloat16)


def finish(scalars, offset, result, pieces, rows, steps):
    tokens = rows * steps
    return pl.pallas_call(
        functools.partial(finish_kernel, pieces, tokens),
        out_shape=(
            jax.ShapeDtypeStruct((rows, steps, GROUP * LANES), jnp.bfloat16),
            jax.ShapeDtypeStruct((pieces, LANES), jnp.float32),
        ),
        in_specs=[pl.BlockSpec(memory_space=pltpu.SMEM)] * 2 + [vmem()],
        out_specs=(vmem(), vmem()),
        compiler_params=pltpu.CompilerParams(vmem_limit_bytes=16 << 20),
        name="finish",
    )(scalars, offset, result)


def exchange(message):
    return lax.all_to_all(message, MP, 0, 0)


def shift(value, stage, step):
    pairs = []
    for core in range(2):
        for x in range(4):
            for z in range(4):
                along_x = core != stage
                to = ((x + step) % 4 if along_x else x) * 4 + (z if along_x else (z + step) % 4)
                pairs.append((core * 16 + x * 4 + z, core * 16 + to))
    return lax.ppermute(value, ("core", "x", "z"), pairs)


def around(value, stage):
    half = value.shape[0] // 2
    right, left = shift(value, stage, 1), shift(value, stage, -1)
    return (value, right, left, shift(right[:half], stage, 1), shift(left[half:], stage, -1))


def across(value, pairs):
    return lax.ppermute(value, ("yhi", "ylo"), [pair for i, j in pairs for pair in ((i, j), (j, i))])


def gather_layer(w_value, message, most):
    columns = w_value.shape[1] // 2
    own = lax.dynamic_slice_in_dim(w_value, lax.axis_index("core") * columns, columns, axis=1)
    plane = jnp.concatenate(around(own, 0), axis=0)
    half = plane.shape[0] // 2
    right, left = shift(plane, 1, 1), shift(plane, 1, -1)
    ahead, behind, message, most = lax.optimization_barrier((right[:half], left[half:], message, most))
    near = (plane, right, left)
    ahead = shift(ahead, 1, 1)
    behind = shift(behind, 1, -1)
    rest = (ahead, behind)
    outer, inner = ((1, 2), (3, 0)), ((0, 1), (2, 3))
    others = (across(plane, outer),)
    others += (across(right, outer), across(left, outer)) + tuple(across(v, inner) for v in rest)
    mine = near + rest + others
    return mine + tuple(lax.ppermute(v, "core", [(0, 1), (1, 0)]) for v in mine), message, most


def per_device(
    step_ids,
    prompt_lens,
    embed_table,
    attn_gain,
    w_qkv,
    w_out,
    key_cache,
    value_cache,
    reward_pieces,
    piece_lens,
    reward_gain,
    w_value,
    b_value,
    w_score,
    b_score,
):
    rows, steps = step_ids.shape
    tokens = rows * steps
    me = lax.axis_index(MP)
    place = jnp.stack([lax.axis_index(name) for name in ("core", "x", "z", "ylo")]).astype(jnp.int32)
    bias = b_value.reshape(4, COLS)
    score = w_score.reshape(4, COLS)

    half_dim = LANES // 2
    frequency = 10000.0 ** (-2.0 * jnp.arange(half_dim, dtype=jnp.float32) / (2 * half_dim))
    positions = (prompt_lens[:, None] + jnp.arange(steps, dtype=jnp.int32)[None, :]).reshape(tokens)
    angles = positions.astype(jnp.float32)[:, None] * frequency
    cos = jnp.concatenate([jnp.cos(angles)] * 2, axis=-1)
    sin = jnp.concatenate([-jnp.sin(angles), jnp.sin(angles)], axis=-1)
    lens = jnp.broadcast_to(jnp.repeat(prompt_lens, steps)[:, None], (tokens, LANES))
    pieces, length, _ = reward_pieces.shape
    total = jnp.sum((piece_lens + (LANES - 1)) // LANES)
    most = jnp.full((8, LANES), total, jnp.int32).astype(jnp.float32)
    for axis in ("core", "yhi"):
        most = jnp.maximum(most, lax.ppermute(most, axis, [(0, 1), (1, 0)]))
    base = length // LANES * pieces // GROUP // 2
    message = pack_first(base, piece_lens, reward_pieces, step_ids, embed_table)
    parts, message, most = gather_layer(w_value, message, most)
    rest = jnp.clip((most[0, 0].astype(jnp.int32) + (GROUP - 1)) // GROUP - base, 0, base)
    first = exchange(message)
    partial = attention(
        first,
        base * LANES,
        tokens,
        attn_gain.astype(jnp.float32).reshape(GROUP, LANES),
        w_qkv,
        cos,
        sin,
        lens,
        key_cache.reshape(rows, -1, LANES),
        value_cache.reshape(rows, -1, LANES),
        w_out,
    )
    gain = reward_gain.astype(jnp.float32).reshape(GROUP, LANES)

    def remainder(slots, first, partial, place, piece_lens, reward_pieces, gain, bias, score, parts):
        second = exchange(pack_rest(base, slots, piece_lens, reward_pieces, partial))
        scored = [score_rows(first, base, place, parts, gain, bias, score)]
        if slots:
            scored.append(score_rows(second, slots, place, parts, gain, bias, score))
        return combine(second, slots * LANES, base, tokens, scored)

    payload = lax.switch(
        rest,
        [functools.partial(remainder, slots) for slots in range(base + 1)],
        first,
        partial,
        place,
        piece_lens,
        reward_pieces,
        gain,
        bias,
        score,
        parts,
    )
    scalars = jnp.concatenate([piece_lens, me.reshape(1).astype(jnp.int32)])
    attn_out, piece_values = finish(scalars, b_score, exchange(payload), pieces, rows, steps)
    return (attn_out, piece_values)


def solution(mesh):
    fine = Mesh(mesh.devices.reshape(2, 2, 4, 4, 2), DP + MP)
    return jax.shard_map(
        per_device,
        mesh=fine,
        in_specs=(
            P(DP, None),
            P(DP),
            P(None, MP),
            P(),
            P(None, None, MP),
            P(MP, None),
            P(DP, MP, None, None),
            P(DP, MP, None, None),
            P(DP, None, MP),
            P(DP),
            P(),
            P(MP, None),
            P(),
            P(),
            P(),
        ),
        out_specs=(P(DP, None, None), P(DP, MP)),
        check_vma=False,
    )
```

profile of v0, /device:TPU:0, one launch (start us, length us, event | category | flops | bytes accessed | tf_op | source)
XLA Modules:
  0.0 219.6 jit_solution(9768203597426092355)
XLA Ops:
  0.6 1.7 constant_dynamic-update-slice_fusion.4
  2.4 2.0 collective-permute-start
  4.4 2.1 collective-permute-start.1
  6.5 4.3 %collective-permute-done = bf16[128,1024]{1,0:T(8,128)(2,1)S(1)} collective-permute-done((bf16[128,1024]{1,0:T(8,128)(2,1)S(1)}, bf16[128,1024]{1,0:T(8,128)(2,1)S(1)}, u32[]{:S(2)}, u32[]{:S(2)}) %collective-permute-start) | collective-permute-done | bytes 262176 | tf_op jit(solution)/shard_map/ppermute | solution.py:394
  11.0 3.3 %collective-permute-start.3 = (bf16[64,1024]{1,0:T(8,128)(2,1)S(1)}, bf16[64,1024]{1,0:T(8,128)(2,1)S(1)}, u32[]{:S(2)}, u32[]{:S(2)}) collective-permute-start(bf16[64,1024]{1,0:T(8,128)(2,1)S(1)} %slice.21), channel_id=1, source_target_pairs={{0,6},{2,0},{4,2},{6,4},{8,14},{10,8},{12,10},{14,12},{16,22},{18,... | collective-permute-start | bytes 393224 | tf_op jit(solution)/shard_map/ppermute | solution.py:394
  15.7 1.4 collective-permute-done.2
  18.4 1.5 collective-permute-start.4
  19.9 1.7 collective-permute-start.5
  24.9 3.2 %collective-permute-start.7 = (f32[8,128]{1,0:T(8,128)S(1)}, f32[8,128]{1,0:T(8,128)S(1)}, u32[]{:S(2)}, u32[]{:S(2)}) collective-permute-start(f32[8,128]{1,0:T(8,128)S(1)} %broadcast_maximum_fusion), channel_id=1, source_target_pairs={{0,64},{64,0},{1,65},{65,1},{2,66},{66,2},{3,67},{67,3},{4,68},{68... | collective-permute-start | bytes 12296 | tf_op jit(solution)/shard_map/ppermute | solution.py:460
  28.1 1.3 copy.18.refs_0_
  29.4 5.4 %shard_map.158 = bf16[32,544,128]{2,1,0:T(8,128)(2,1)} custom-call(s32[8]{0:T(128)} %lens_ref.1, bf16[8,4096,128]{2,1,0:T(8,128)(2,1)} %pieces_ref.1, s32[8,4]{1,0:T(8,128)} %copy.18.refs_0_, bf16[32000,128]{1,0:T(8,128)(2,1)} %refs_1_.1), custom_call_target="tpu_custom_call" | custom-call | bytes 8912896 | tf_op jit(solution)/shard_map/pallas_call | solution.py:329
  35.8 1.9 slice.23
  37.7 7.3 %all-to-all-start.5 = ((bf16[32,544,128]{2,1,0:T(8,128)(2,1)}), bf16[32,544,128]{2,1,0:T(8,128)(2,1)}, u32[]{:S(2)}, u32[]{:S(2)}) async-start(bf16[32,544,128]{2,1,0:T(8,128)(2,1)} %shard_map.158), calls=%async_computation.5 | async-start | bytes 8912896 | tf_op jit(solution)/shard_map/all_to_all | solution.py:383
  44.9 3.2 %collective-permute-start.10 = (bf16[512,1024]{1,0:T(8,128)(2,1)}, bf16[512,1024]{1,0:T(8,128)(2,1)}, u32[]{:S(2)}, u32[]{:S(2)}) collective-permute-start(bf16[512,1024]{1,0:T(8,128)(2,1)} %constant_dynamic-update-slice_fusion), channel_id=1, source_target_pairs={{1,64},{64,1},{65,0},{0,65},{3,66},{66,3},{67,2},{2,67},{5,68},{68... | collective-permute-start | bytes 3145736 | tf_op jit(solution)/shard_map/ppermute | solution.py:404
  48.4 1.6 collective-permute-start.8
  50.0 2.9 %collective-permute-start.12 = (bf16[512,1024]{1,0:T(8,128)(2,1)}, bf16[512,1024]{1,0:T(8,128)(2,1)}, u32[]{:S(2)}, u32[]{:S(2)}) collective-permute-start(bf16[512,1024]{1,0:T(8,128)(2,1)} %collective-permute-done.5), channel_id=1, source_target_pairs={{1,64},{64,1},{65,0},{0,65},{3,66},{66,3},{67,2},{2,67},{5,68},{68... | collective-permute-start | bytes 3145736 | tf_op jit(solution)/shard_map/ppermute | solution.py:404
  52.9 19.7 %collective-permute-done.10 = bf16[512,1024]{1,0:T(8,128)(2,1)} collective-permute-done((bf16[512,1024]{1,0:T(8,128)(2,1)}, bf16[512,1024]{1,0:T(8,128)(2,1)}, u32[]{:S(2)}, u32[]{:S(2)}) %collective-permute-start.10) | collective-permute-done | bytes 1048608 | tf_op jit(solution)/shard_map/ppermute | solution.py:404
  72.6 3.0 %collective-permute-start.9 = (bf16[256,1024]{1,0:T(8,128)(2,1)}, bf16[256,1024]{1,0:T(8,128)(2,1)}, u32[]{:S(2)}, u32[]{:S(2)}) collective-permute-start(bf16[256,1024]{1,0:T(8,128)(2,1)} %slice.23), channel_id=1, source_target_pairs={{0,24},{2,26},{4,28},{6,30},{8,0},{10,2},{12,4},{14,6},{16,8},{18,... | collective-permute-start | bytes 1572872 | tf_op jit(solution)/shard_map/ppermute | solution.py:394
  75.6 27.1 %collective-permute-done.8 = bf16[256,1024]{1,0:T(8,128)(2,1)S(1)} collective-permute-done((bf16[256,1024]{1,0:T(8,128)(2,1)}, bf16[256,1024]{1,0:T(8,128)(2,1)S(1)}, u32[]{:S(2)}, u32[]{:S(2)}) %collective-permute-start.8) | collective-permute-done | bytes 524320 | tf_op jit(solution)/shard_map/ppermute | solution.py:394
  105.8 9.0 %collective-permute-done.12 = bf16[512,1024]{1,0:T(8,128)(2,1)} collective-permute-done((bf16[512,1024]{1,0:T(8,128)(2,1)}, bf16[512,1024]{1,0:T(8,128)(2,1)}, u32[]{:S(2)}, u32[]{:S(2)}) %collective-permute-start.12) | collective-permute-done | bytes 1048608 | tf_op jit(solution)/shard_map/ppermute | solution.py:404
  114.8 3.6 %collective-permute-done.13 = bf16[256,1024]{1,0:T(8,128)(2,1)} collective-permute-done((bf16[256,1024]{1,0:T(8,128)(2,1)S(1)}, bf16[256,1024]{1,0:T(8,128)(2,1)}, u32[]{:S(2)}, u32[]{:S(2)}) %collective-permute-start.13) | collective-permute-done | bytes 524320 | tf_op jit(solution)/shard_map/ppermute | solution.py:404
  118.4 10.0 %collective-permute-done.14 = bf16[256,1024]{1,0:T(8,128)(2,1)} collective-permute-done((bf16[256,1024]{1,0:T(8,128)(2,1)}, bf16[256,1024]{1,0:T(8,128)(2,1)}, u32[]{:S(2)}, u32[]{:S(2)}) %collective-permute-start.14) | collective-permute-done | bytes 524320 | tf_op jit(solution)/shard_map/ppermute | solution.py:404
  133.1 5.2 %attention.1 = bf16[64,4096]{1,0:T(8,128)(2,1)S(1)} custom-call(bf16[32,544,128]{2,1,0:T(8,128)(2,1)} %all-to-all-done.5.message_ref, f32[32,128]{1,0:T(8,128)} %bitcast_convert_fusion.1.gain_ref, bf16[3,4096,128]{2,1,0:T(8,128)(2,1)} %wqkv_hbm.1, f32[32,128]{1,0:T(8,128)} %get-tuple-element.441.cos_ref, f32[32,128]{1,0:T(8,128)} %get-tuple-element.442.sin_ref, ...), custom_call_target="tpu_custom_call" | custom-call | flops 400000000 | bytes 9437184 | tf_op jit(solution)/shard_map/attention/pallas_call | solution.py:107
  138.3 59.0 %conditional.1 = (f32[32,40,128]{2,1,0:T(8,128)}) conditional(s32[]{:T(128)} %clamp.3, (s32[8]{0:T(128)S(1)}, bf16[8,4096,128]{2,1,0:T(8,128)(2,1)}, bf16[64,4096]{1,0:T(8,128)(2,1)S(1)}, s32[4]{0:T(128)S(1)}, bf16[32,544,128]{2,1,0:T(8,128)(2,1)}, /*index=5*/bf16[512,1024]{1,0:T(8,128)(2,1)}, ...), branch_computations={%region_1.2_spmd, %region_2.3_spmd, %region_3.4_spmd, %region_4.5_... | conditional | flops 17179969536 | bytes 76546120 | solution.py:488
  138.5 4.4 %branch_2_fun.1 = bf16[32,320,128]{2,1,0:T(8,128)(2,1)} custom-call(s32[8]{0:T(128)S(1)} %get-tuple-element.342.lens_ref, bf16[8,4096,128]{2,1,0:T(8,128)(2,1)} %get-tuple-element.343.pieces_ref, bf16[64,4096]{1,0:T(8,128)(2,1)S(1)} %get-tuple-element.344.refs_0_), custom_call_target="tpu_custom_call" | custom-call | bytes 5242880 | tf_op jit(solution)/shard_map/cond/branch_2_fun/pallas_call | solution.py:329
  143.0 7.0 %all-to-all-start.2 = ((bf16[32,320,128]{2,1,0:T(8,128)(2,1)}), bf16[32,320,128]{2,1,0:T(8,128)(2,1)}, u32[]{:S(2)}, u32[]{:S(2)}) async-start(bf16[32,320,128]{2,1,0:T(8,128)(2,1)} %branch_2_fun.1), calls=%async_computation.2 | async-start | bytes 5242880 | tf_op jit(solution)/shard_map/cond/branch_2_fun/all_to_all | solution.py:383
  150.0 16.6 %score.12.refs_0_ = f32[4,128]{1,0:T(4,128)} custom-call(s32[4]{0:T(128)S(1)} %get-tuple-element.345.place_ref, bf16[32,544,128]{2,1,0:T(8,128)(2,1)} %get-tuple-element.346.x_hbm, bf16[512,1024]{1,0:T(8,128)(2,1)} %get-tuple-element.347.refs_0_, bf16[512,1024]{1,0:T(8,128)(2,1)S(1)} %get-tuple-element.348.refs_1_, ...), custom_call_target="tpu_custom_call" | custom-call | flops 8589934592 | bytes 25165824 | tf_op jit(solution)/shard_map/cond/branch_2_fun/score/pallas_call | solution.py:236
  166.6 17.4 %all-to-all-done.2.x_hbm.message_ref = bf16[32,320,128]{2,1,0:T(8,128)(2,1)} async-done(((bf16[32,320,128]{2,1,0:T(8,128)(2,1)}), bf16[32,320,128]{2,1,0:T(8,128)(2,1)}, u32[]{:S(2)}, u32[]{:S(2)}) %all-to-all-start.2) | async-done | bytes 2621472 | tf_op jit(solution)/shard_map/cond/branch_2_fun/all_to_all | solution.py:383
  184.0 10.3 %score.13.refs_1_ = f32[2,128]{1,0:T(2,128)} custom-call(s32[4]{0:T(128)S(1)} %get-tuple-element.345.place_ref, bf16[32,320,128]{2,1,0:T(8,128)(2,1)} %all-to-all-done.2.x_hbm.message_ref, bf16[512,1024]{1,0:T(8,128)(2,1)} %get-tuple-element.347.refs_0_, bf16[512,1024]{1,0:T(8,128)(2,1)S(1)} %get-tuple-element.348.refs_1_, ...), custom_call_target="tpu_custom_call" | custom-call | flops 4294967296 | bytes 25165824 | tf_op jit(solution)/shard_map/cond/branch_2_fun/score/pallas_call | solution.py:236
  194.3 2.7 %combine.7 = f32[32,40,128]{2,1,0:T(8,128)} custom-call(bf16[32,320,128]{2,1,0:T(8,128)(2,1)} %all-to-all-done.2.x_hbm.message_ref, f32[4,128]{1,0:T(4,128)} %score.12.refs_0_, f32[2,128]{1,0:T(2,128)} %score.13.refs_1_), custom_call_target="tpu_custom_call" | custom-call | flops 100000 | bytes 524288 | tf_op jit(solution)/shard_map/cond/branch_2_fun/combine/pallas_call | solution.py:142
  197.3 7.3 %all-to-all-start.6 = ((f32[32,40,128]{2,1,0:T(8,128)}), f32[32,40,128]{2,1,0:T(8,128)S(1)}, u32[]{:S(2)}, u32[]{:S(2)}) async-start(f32[32,40,128]{2,1,0:T(8,128)} %get-tuple-element.443), calls=%async_computation.6 | async-start | bytes 1310720 | tf_op jit(solution)/shard_map/all_to_all | solution.py:383
  205.4 12.9 %all-to-all-done.6.result_ref = f32[32,40,128]{2,1,0:T(8,128)S(1)} async-done(((f32[32,40,128]{2,1,0:T(8,128)}), f32[32,40,128]{2,1,0:T(8,128)S(1)}, u32[]{:S(2)}, u32[]{:S(2)}) %all-to-all-start.6) | async-done | bytes 655392 | tf_op jit(solution)/shard_map/all_to_all | solution.py:383
  (82 shorter events, 15.0 us)
Async XLA Ops:
  2.4 8.5 %collective-permute-start = (bf16[128,1024]{1,0:T(8,128)(2,1)S(1)}, bf16[128,1024]{1,0:T(8,128)(2,1)S(1)}, u32[]{:S(2)}, u32[]{:S(2)}) collective-permute-start(bf16[128,1024]{1,0:T(8,128)(2,1)S(1)} %get-tuple-element.437), channel_id=1, source_target_pairs={{0,2},{2,4},{4,6},{6,0},{8,10},{10,12},{12,14},{14,8},{16,18},{18,... | collective-permute-start | bytes 786440 | tf_op jit(solution)/shard_map/ppermute | solution.py:394
  4.4 6.6 %collective-permute-start.1 = (bf16[128,1024]{1,0:T(8,128)(2,1)S(1)}, bf16[128,1024]{1,0:T(8,128)(2,1)S(1)}, u32[]{:S(2)}, u32[]{:S(2)}) collective-permute-start(bf16[128,1024]{1,0:T(8,128)(2,1)S(1)} %get-tuple-element.437), channel_id=1, source_target_pairs={{0,6},{2,0},{4,2},{6,4},{8,14},{10,8},{12,10},{14,12},{16,22},{18,... | collective-permute-start | bytes 786440 | tf_op jit(solution)/shard_map/ppermute | solution.py:394
  10.9 6.2 %collective-permute-start.2 = (bf16[64,1024]{1,0:T(8,128)(2,1)S(1)}, bf16[64,1024]{1,0:T(8,128)(2,1)S(1)}, u32[]{:S(2)}, u32[]{:S(2)}) collective-permute-start(bf16[64,1024]{1,0:T(8,128)(2,1)S(1)} %slice.20), channel_id=1, source_target_pairs={{0,2},{2,4},{4,6},{6,0},{8,10},{10,12},{12,14},{14,8},{16,18},{18,... | collective-permute-start | bytes 393224 | tf_op jit(solution)/shard_map/ppermute | solution.py:394
  11.0 6.8 %collective-permute-start.3 = (bf16[64,1024]{1,0:T(8,128)(2,1)S(1)}, bf16[64,1024]{1,0:T(8,128)(2,1)S(1)}, u32[]{:S(2)}, u32[]{:S(2)}) collective-permute-start(bf16[64,1024]{1,0:T(8,128)(2,1)S(1)} %slice.21), channel_id=1, source_target_pairs={{0,6},{2,0},{4,2},{6,4},{8,14},{10,8},{12,10},{14,12},{16,22},{18,... | collective-permute-start | bytes 393224 | tf_op jit(solution)/shard_map/ppermute | solution.py:394
  18.4 16.5 %collective-permute-start.4 = (bf16[512,1024]{1,0:T(8,128)(2,1)}, bf16[512,1024]{1,0:T(8,128)(2,1)S(1)}, u32[]{:S(2)}, u32[]{:S(2)}) collective-permute-start(bf16[512,1024]{1,0:T(8,128)(2,1)} %constant_dynamic-update-slice_fusion), channel_id=1, source_target_pairs={{0,8},{2,10},{4,12},{6,14},{8,16},{10,18},{12,20},{14,22},{16,24},... | collective-permute-start | bytes 3145736 | tf_op jit(solution)/shard_map/ppermute | solution.py:394
  19.9 15.8 %collective-permute-start.5 = (bf16[512,1024]{1,0:T(8,128)(2,1)}, bf16[512,1024]{1,0:T(8,128)(2,1)}, u32[]{:S(2)}, u32[]{:S(2)}) collective-permute-start(bf16[512,1024]{1,0:T(8,128)(2,1)} %constant_dynamic-update-slice_fusion), channel_id=1, source_target_pairs={{0,24},{2,26},{4,28},{6,30},{8,0},{10,2},{12,4},{14,6},{16,8},{18,... | collective-permute-start | bytes 3145736 | tf_op jit(solution)/shard_map/ppermute | solution.py:394
  23.6 1.2 collective-permute-start.6
  24.9 10.0 %collective-permute-start.7 = (f32[8,128]{1,0:T(8,128)S(1)}, f32[8,128]{1,0:T(8,128)S(1)}, u32[]{:S(2)}, u32[]{:S(2)}) collective-permute-start(f32[8,128]{1,0:T(8,128)S(1)} %broadcast_maximum_fusion), channel_id=1, source_target_pairs={{0,64},{64,0},{1,65},{65,1},{2,66},{66,2},{3,67},{67,3},{4,68},{68... | collective-permute-start | bytes 12296 | tf_op jit(solution)/shard_map/ppermute | solution.py:460
  37.6 92.9 %copy-start.12 = (f32[2048]{0:T(1024)S(1)}, f32[2048]{0:T(1024)}, u32[]{:S(2)}) copy-start(f32[2048]{0:T(1024)} %param.32) | copy-start | bytes 24580
  37.6 92.9 %copy-start.13 = (f32[2048]{0:T(1024)S(1)}, f32[2048]{0:T(1024)}, u32[]{:S(2)}) copy-start(f32[2048]{0:T(1024)} %param.33) | copy-start | bytes 24580
  37.6 92.9 %copy-start.10 = (bf16[4096]{0:T(1024)(128)(2,1)S(1)}, bf16[4096]{0:T(1024)(128)(2,1)}, u32[]{:S(2)}) copy-start(bf16[4096]{0:T(1024)(128)(2,1)} %param.23) | copy-start | bytes 24580
  37.6 93.5 %copy-start.11 = (bf16[4096]{0:T(1024)(128)(2,1)S(1)}, bf16[4096]{0:T(1024)(128)(2,1)}, u32[]{:S(2)}) copy-start(bf16[4096]{0:T(1024)(128)(2,1)} %param.30) | copy-start | bytes 24580
  37.7 94.7 %all-to-all-start.5 = ((bf16[32,544,128]{2,1,0:T(8,128)(2,1)}), bf16[32,544,128]{2,1,0:T(8,128)(2,1)}, u32[]{:S(2)}, u32[]{:S(2)}) async-start(bf16[32,544,128]{2,1,0:T(8,128)(2,1)} %shard_map.158), calls=%async_computation.5 | async-start | bytes 8912896 | tf_op jit(solution)/shard_map/all_to_all | solution.py:383
  44.9 27.6 %collective-permute-start.10 = (bf16[512,1024]{1,0:T(8,128)(2,1)}, bf16[512,1024]{1,0:T(8,128)(2,1)}, u32[]{:S(2)}, u32[]{:S(2)}) collective-permute-start(bf16[512,1024]{1,0:T(8,128)(2,1)} %constant_dynamic-update-slice_fusion), channel_id=1, source_target_pairs={{1,64},{64,1},{65,0},{0,65},{3,66},{66,3},{67,2},{2,67},{5,68},{68... | collective-permute-start | bytes 3145736 | tf_op jit(solution)/shard_map/ppermute | solution.py:404
  48.2 27.4 %collective-permute-start.15 = (bf16[512,1024]{1,0:T(8,128)(2,1)}, bf16[512,1024]{1,0:T(8,128)(2,1)S(1)}, u32[]{:S(2)}, u32[]{:S(2)}) collective-permute-start(bf16[512,1024]{1,0:T(8,128)(2,1)} %constant_dynamic-update-slice_fusion), channel_id=1, source_target_pairs={{0,32},{32,0},{1,33},{33,1},{2,34},{34,2},{3,35},{35,3},{4,36},{36... | collective-permute-start | bytes 3145736 | tf_op jit(solution)/shard_map/ppermute | solution.py:422
  48.2 56.4 %collective-permute-start.11 = (bf16[512,1024]{1,0:T(8,128)(2,1)S(1)}, bf16[512,1024]{1,0:T(8,128)(2,1)}, u32[]{:S(2)}, u32[]{:S(2)}) collective-permute-start(bf16[512,1024]{1,0:T(8,128)(2,1)S(1)} %collective-permute-done.4), channel_id=1, source_target_pairs={{1,64},{64,1},{65,0},{0,65},{3,66},{66,3},{67,2},{2,67},{5,68},{68... | collective-permute-start | bytes 3145736 | tf_op jit(solution)/shard_map/ppermute | solution.py:404
  48.4 54.3 %collective-permute-start.8 = (bf16[256,1024]{1,0:T(8,128)(2,1)}, bf16[256,1024]{1,0:T(8,128)(2,1)S(1)}, u32[]{:S(2)}, u32[]{:S(2)}) collective-permute-start(bf16[256,1024]{1,0:T(8,128)(2,1)} %slice.22), channel_id=1, source_target_pairs={{0,8},{2,10},{4,12},{6,14},{8,16},{10,18},{12,20},{14,22},{16,24},... | collective-permute-start | bytes 1572872 | tf_op jit(solution)/shard_map/ppermute | solution.py:394
  50.0 64.8 %collective-permute-start.12 = (bf16[512,1024]{1,0:T(8,128)(2,1)}, bf16[512,1024]{1,0:T(8,128)(2,1)}, u32[]{:S(2)}, u32[]{:S(2)}) collective-permute-start(bf16[512,1024]{1,0:T(8,128)(2,1)} %collective-permute-done.5), channel_id=1, source_target_pairs={{1,64},{64,1},{65,0},{0,65},{3,66},{66,3},{67,2},{2,67},{5,68},{68... | collective-permute-start | bytes 3145736 | tf_op jit(solution)/shard_map/ppermute | solution.py:404
  72.6 31.0 %collective-permute-start.9 = (bf16[256,1024]{1,0:T(8,128)(2,1)}, bf16[256,1024]{1,0:T(8,128)(2,1)}, u32[]{:S(2)}, u32[]{:S(2)}) collective-permute-start(bf16[256,1024]{1,0:T(8,128)(2,1)} %slice.23), channel_id=1, source_target_pairs={{0,24},{2,26},{4,28},{6,30},{8,0},{10,2},{12,4},{14,6},{16,8},{18,... | collective-permute-start | bytes 1572872 | tf_op jit(solution)/shard_map/ppermute | solution.py:394
  75.6 52.9 %collective-permute-start.16 = (bf16[512,1024]{1,0:T(8,128)(2,1)S(1)}, bf16[512,1024]{1,0:T(8,128)(2,1)S(1)}, u32[]{:S(2)}, u32[]{:S(2)}) collective-permute-start(bf16[512,1024]{1,0:T(8,128)(2,1)S(1)} %collective-permute-done.4), channel_id=1, source_target_pairs={{0,32},{32,0},{1,33},{33,1},{2,34},{34,2},{3,35},{35,3},{4,36},{36... | collective-permute-start | bytes 3145736 | tf_op jit(solution)/shard_map/ppermute | solution.py:422
  102.7 26.3 %collective-permute-start.17 = (bf16[512,1024]{1,0:T(8,128)(2,1)}, bf16[512,1024]{1,0:T(8,128)(2,1)}, u32[]{:S(2)}, u32[]{:S(2)}) collective-permute-start(bf16[512,1024]{1,0:T(8,128)(2,1)} %collective-permute-done.5), channel_id=1, source_target_pairs={{0,32},{32,0},{1,33},{33,1},{2,34},{34,2},{3,35},{35,3},{4,36},{36... | collective-permute-start | bytes 3145736 | tf_op jit(solution)/shard_map/ppermute | solution.py:422
  103.5 14.9 %collective-permute-start.13 = (bf16[256,1024]{1,0:T(8,128)(2,1)S(1)}, bf16[256,1024]{1,0:T(8,128)(2,1)}, u32[]{:S(2)}, u32[]{:S(2)}) collective-permute-start(bf16[256,1024]{1,0:T(8,128)(2,1)S(1)} %collective-permute-done.8), channel_id=1, source_target_pairs={{0,1},{1,0},{64,65},{65,64},{2,3},{3,2},{66,67},{67,66},{4,5},{5,4... | collective-permute-start | bytes 1572872 | tf_op jit(solution)/shard_map/ppermute | solution.py:404
  104.6 23.8 %collective-permute-start.14 = (bf16[256,1024]{1,0:T(8,128)(2,1)}, bf16[256,1024]{1,0:T(8,128)(2,1)}, u32[]{:S(2)}, u32[]{:S(2)}) collective-permute-start(bf16[256,1024]{1,0:T(8,128)(2,1)} %collective-permute-done.9), channel_id=1, source_target_pairs={{0,1},{1,0},{64,65},{65,64},{2,3},{3,2},{66,67},{67,66},{4,5},{5,4... | collective-permute-start | bytes 1572872 | tf_op jit(solution)/shard_map/ppermute | solution.py:404
  114.8 15.1 %collective-permute-start.18 = (bf16[256,1024]{1,0:T(8,128)(2,1)S(1)}, bf16[256,1024]{1,0:T(8,128)(2,1)}, u32[]{:S(2)}, u32[]{:S(2)}) collective-permute-start(bf16[256,1024]{1,0:T(8,128)(2,1)S(1)} %collective-permute-done.8), channel_id=1, source_target_pairs={{0,32},{32,0},{1,33},{33,1},{2,34},{34,2},{3,35},{35,3},{4,36},{36... | collective-permute-start | bytes 1572872 | tf_op jit(solution)/shard_map/ppermute | solution.py:422
  118.4 11.9 %collective-permute-start.19 = (bf16[256,1024]{1,0:T(8,128)(2,1)}, bf16[256,1024]{1,0:T(8,128)(2,1)}, u32[]{:S(2)}, u32[]{:S(2)}) collective-permute-start(bf16[256,1024]{1,0:T(8,128)(2,1)} %collective-permute-done.9), channel_id=1, source_target_pairs={{0,32},{32,0},{1,33},{33,1},{2,34},{34,2},{3,35},{35,3},{4,36},{36... | collective-permute-start | bytes 1572872 | tf_op jit(solution)/shard_map/ppermute | solution.py:422
  128.4 9.8 %collective-permute-start.20 = (bf16[512,1024]{1,0:T(8,128)(2,1)}, bf16[512,1024]{1,0:T(8,128)(2,1)}, u32[]{:S(2)}, u32[]{:S(2)}) collective-permute-start(bf16[512,1024]{1,0:T(8,128)(2,1)} %collective-permute-done.10), channel_id=1, source_target_pairs={{0,32},{32,0},{1,33},{33,1},{2,34},{34,2},{3,35},{35,3},{4,36},{36... | collective-permute-start | bytes 3145736 | tf_op jit(solution)/shard_map/ppermute | solution.py:422
  128.4 9.8 %collective-permute-start.21 = (bf16[512,1024]{1,0:T(8,128)(2,1)}, bf16[512,1024]{1,0:T(8,128)(2,1)}, u32[]{:S(2)}, u32[]{:S(2)}) collective-permute-start(bf16[512,1024]{1,0:T(8,128)(2,1)} %collective-permute-done.11), channel_id=1, source_target_pairs={{0,32},{32,0},{1,33},{33,1},{2,34},{34,2},{3,35},{35,3},{4,36},{36... | collective-permute-start | bytes 3145736 | tf_op jit(solution)/shard_map/ppermute | solution.py:422
  129.0 9.3 %collective-permute-start.22 = (bf16[512,1024]{1,0:T(8,128)(2,1)}, bf16[512,1024]{1,0:T(8,128)(2,1)}, u32[]{:S(2)}, u32[]{:S(2)}) collective-permute-start(bf16[512,1024]{1,0:T(8,128)(2,1)} %collective-permute-done.12), channel_id=1, source_target_pairs={{0,32},{32,0},{1,33},{33,1},{2,34},{34,2},{3,35},{35,3},{4,36},{36... | collective-permute-start | bytes 3145736 | tf_op jit(solution)/shard_map/ppermute | solution.py:422
  129.9 8.3 %collective-permute-start.23 = (bf16[256,1024]{1,0:T(8,128)(2,1)}, bf16[256,1024]{1,0:T(8,128)(2,1)}, u32[]{:S(2)}, u32[]{:S(2)}) collective-permute-start(bf16[256,1024]{1,0:T(8,128)(2,1)} %collective-permute-done.13), channel_id=1, source_target_pairs={{0,32},{32,0},{1,33},{33,1},{2,34},{34,2},{3,35},{35,3},{4,36},{36... | collective-permute-start | bytes 1572872 | tf_op jit(solution)/shard_map/ppermute | solution.py:422
  130.3 7.9 %collective-permute-start.24 = (bf16[256,1024]{1,0:T(8,128)(2,1)}, bf16[256,1024]{1,0:T(8,128)(2,1)}, u32[]{:S(2)}, u32[]{:S(2)}) collective-permute-start(bf16[256,1024]{1,0:T(8,128)(2,1)} %collective-permute-done.14), channel_id=1, source_target_pairs={{0,32},{32,0},{1,33},{33,1},{2,34},{34,2},{3,35},{35,3},{4,36},{36... | collective-permute-start | bytes 1572872 | tf_op jit(solution)/shard_map/ppermute | solution.py:422
  143.0 41.1 %all-to-all-start.2 = ((bf16[32,320,128]{2,1,0:T(8,128)(2,1)}), bf16[32,320,128]{2,1,0:T(8,128)(2,1)}, u32[]{:S(2)}, u32[]{:S(2)}) async-start(bf16[32,320,128]{2,1,0:T(8,128)(2,1)} %branch_2_fun.1), calls=%async_computation.2 | async-start | bytes 5242880 | tf_op jit(solution)/shard_map/cond/branch_2_fun/all_to_all | solution.py:383
  197.3 20.9 %all-to-all-start.6 = ((f32[32,40,128]{2,1,0:T(8,128)}), f32[32,40,128]{2,1,0:T(8,128)S(1)}, u32[]{:S(2)}, u32[]{:S(2)}) async-start(f32[32,40,128]{2,1,0:T(8,128)} %get-tuple-element.443), calls=%async_computation.6 | async-start | bytes 1310720 | tf_op jit(solution)/shard_map/all_to_all | solution.py:383
  (6 other events, 144.2 us)
where the time goes:
time: 221 us; the launch traced here: 220 us
  waiting for transfers between devices  107 us (48%)
  starting transfers between devices  49.7 us (22%)
  Pallas kernels  45.9 us (21%)
  local copies, waits for them, and re-layouts  10.1 us (5%)
  other arithmetic  2.92 us (1%)
  between operations  2.87 us (1%)
    ppermute x5, waiting for transfers between devices, across(): lax.ppermute(value, ('yhi', 'ylo'), [pair for i, j in pairs for pair in (...  42.3 us
    ppermute x8, waiting for transfers between devices, shift(): return lax.ppermute(value, ('core', 'x', 'z'), pairs)  33.7 us
    all_to_all x3, waiting for transfers between devices, exchange(): return lax.all_to_all(message, MP, 0, 0)  30.3 us
    pallas_call x2, Pallas kernels, score_rows(): pl.pallas_call(functools.partial(score_kernel, slots), out_shape=jax.Shap...  26.9 us
    all_to_all x3, starting transfers between devices, exchange(): return lax.all_to_all(message, MP, 0, 0)  21.6 us
    ppermute x8, starting transfers between devices, shift(): return lax.ppermute(value, ('core', 'x', 'z'), pairs)  15.3 us
    pallas_call x2, Pallas kernels, pack(): pl.pallas_call(functools.partial(pack_kernel, operands[1].shape[0], first...  9.84 us
    ppermute x5, starting transfers between devices, across(): lax.ppermute(value, ('yhi', 'ylo'), [pair for i, j in pairs for pair in (...  8.35 us
  transfers between devices with their start and end apart: 28, of which 11 were waited for; matrix products, arithmetic and copies ran while one was open for 4% of the time, Pallas kernels for 12%

commit v1 on v0

--- a/solution.py
+++ b/solution.py
@@ -416,10 +416,14 @@
     behind = shift(behind, 1, -1)
     rest = (ahead, behind)
     outer, inner = ((1, 2), (3, 0)), ((0, 1), (2, 3))
-    others = (across(plane, outer),)
-    others += (across(right, outer), across(left, outer)) + tuple(across(v, inner) for v in rest)
-    mine = near + rest + others
-    return mine + tuple(lax.ppermute(v, "core", [(0, 1), (1, 0)]) for v in mine), message, most
+    others = (across(plane, inner),)
+    others += (across(right, outer),)
+    others += (across(left, outer),) + tuple(across(v, outer) for v in rest)
+    return near + rest + others, message, most
+
+
+def swap_cores(value):
+    return lax.ppermute(value, "core", [(0, 1), (1, 0)])
 
 
 def per_device(
@@ -477,6 +481,9 @@
         w_out,
     )
     gain = reward_gain.astype(jnp.float32).reshape(GROUP, LANES)
+    swapped = tuple(swap_cores(part) for part in parts[:-2])
+    *last, partial = lax.optimization_barrier(parts[-2:] + (partial,))
+    parts = parts + swapped + tuple(swap_cores(part) for part in last)
 
     def remainder(slots, first, partial, place, piece_lens, reward_pieces, gain, bias, score, parts):
         second = exchange(pack_rest(base, slots, piece_lens, reward_pieces, partial))

time: 221 us -> 266 us (1.20)
  waiting for transfers between devices: 107 us -> 153 us
    ppermute x8, waiting for transfers between devices: 33.7 us -> 57.8 us  [shift(): return lax.ppermute(value, ('core', 'x', 'z'), pairs)]
    ppermute x5, waiting for transfers between devices: 42.3 us -> 62.9 us  [across(): lax.ppermute(value, ('yhi', 'ylo'), [pair for i, j in pairs for pair in (...]
  transfers between devices with their start and end apart: 28 -> 28, of which waited for: 11 -> 11; matrix products, arithmetic and copies ran while one was open for 4% -> 3% of each run, Pallas kernels for 12% -> 10%
where the time goes in v1:
time: 266 us; the launch traced here: 265 us
  waiting for transfers between devices  153 us (58%)
  starting transfers between devices  49.9 us (19%)
  Pallas kernels  45.9 us (17%)
  local copies, waits for them, and re-layouts  9.28 us (3%)
  other arithmetic  2.92 us (1%)
  between operations  2.85 us (1%)
    ppermute x5, waiting for transfers between devices, across(): lax.ppermute(value, ('yhi', 'ylo'), [pair for i, j in pairs for pair in (...  62.9 us
    ppermute x8, waiting for transfers between devices, shift(): return lax.ppermute(value, ('core', 'x', 'z'), pairs)  57.8 us
    all_to_all x3, waiting for transfers between devices, exchange(): return lax.all_to_all(message, MP, 0, 0)  30.2 us
    pallas_call x2, Pallas kernels, score_rows(): pl.pallas_call(functools.partial(score_kernel, slots), out_shape=jax.Shap...  26.9 us
    all_to_all x3, starting transfers between devices, exchange(): return lax.all_to_all(message, MP, 0, 0)  22.2 us
    ppermute x8, starting transfers between devices, shift(): return lax.ppermute(value, ('core', 'x', 'z'), pairs)  14 us
    pallas_call x2, Pallas kernels, pack(): pl.pallas_call(functools.partial(pack_kernel, operands[1].shape[0], first...  9.81 us
    ppermute x5, starting transfers between devices, across(): lax.ppermute(value, ('yhi', 'ylo'), [pair for i, j in pairs for pair in (...  8.28 us
  transfers between devices with their start and end apart: 28, of which 11 were waited for; matrix products, arithmetic and copies ran while one was open for 3% of the time, Pallas kernels for 10%

profile of v1, /device:TPU:0, one launch (start us, length us, event | category | flops | bytes accessed | tf_op | source)
XLA Modules:
  0.0 264.6 jit_solution(10413377055577844097)
XLA Ops:
  0.6 1.7 constant_dynamic-update-slice_fusion.4
  2.3 2.0 collective-permute-start
  4.4 2.1 collective-permute-start.1
  6.5 4.3 %collective-permute-done = bf16[128,1024]{1,0:T(8,128)(2,1)S(1)} collective-permute-done((bf16[128,1024]{1,0:T(8,128)(2,1)S(1)}, bf16[128,1024]{1,0:T(8,128)(2,1)S(1)}, u32[]{:S(2)}, u32[]{:S(2)}) %collective-permute-start) | collective-permute-done | bytes 262176 | tf_op jit(solution)/shard_map/ppermute | solution.py:394
  11.0 3.3 %collective-permute-start.3 = (bf16[64,1024]{1,0:T(8,128)(2,1)S(1)}, bf16[64,1024]{1,0:T(8,128)(2,1)S(1)}, u32[]{:S(2)}, u32[]{:S(2)}) collective-permute-start(bf16[64,1024]{1,0:T(8,128)(2,1)S(1)} %slice.21), channel_id=1, source_target_pairs={{0,6},{2,0},{4,2},{6,4},{8,14},{10,8},{12,10},{14,12},{16,22},{18,... | collective-permute-start | bytes 393224 | tf_op jit(solution)/shard_map/ppermute | solution.py:394
  15.7 1.4 collective-permute-done.2
  18.4 1.5 collective-permute-start.4
  19.9 1.7 collective-permute-start.5
  24.9 3.2 %collective-permute-start.7 = (f32[8,128]{1,0:T(8,128)S(1)}, f32[8,128]{1,0:T(8,128)S(1)}, u32[]{:S(2)}, u32[]{:S(2)}) collective-permute-start(f32[8,128]{1,0:T(8,128)S(1)} %broadcast_maximum_fusion), channel_id=1, source_target_pairs={{0,64},{64,0},{1,65},{65,1},{2,66},{66,2},{3,67},{67,3},{4,68},{68... | collective-permute-start | bytes 12296 | tf_op jit(solution)/shard_map/ppermute | solution.py:464
  28.1 1.3 copy.18.refs_0_
  29.4 5.4 %shard_map.158 = bf16[32,544,128]{2,1,0:T(8,128)(2,1)} custom-call(s32[8]{0:T(128)} %lens_ref.1, bf16[8,4096,128]{2,1,0:T(8,128)(2,1)} %pieces_ref.1, s32[8,4]{1,0:T(8,128)} %copy.18.refs_0_, bf16[32000,128]{1,0:T(8,128)(2,1)} %refs_1_.1), custom_call_target="tpu_custom_call" | custom-call | bytes 8912896 | tf_op jit(solution)/shard_map/pallas_call | solution.py:329
  35.0 1.9 slice.23
  36.9 8.0 %all-to-all-start.5 = ((bf16[32,544,128]{2,1,0:T(8,128)(2,1)}), bf16[32,544,128]{2,1,0:T(8,128)(2,1)}, u32[]{:S(2)}, u32[]{:S(2)}) async-start(bf16[32,544,128]{2,1,0:T(8,128)(2,1)} %shard_map.158), calls=%async_computation.5 | async-start | bytes 8912896 | tf_op jit(solution)/shard_map/all_to_all | solution.py:383
  44.9 1.8 collective-permute-start.12
  46.7 1.5 collective-permute-start.8
  48.2 1.8 collective-permute-start.10
  50.0 52.0 %collective-permute-done.8 = bf16[256,1024]{1,0:T(8,128)(2,1)} collective-permute-done((bf16[256,1024]{1,0:T(8,128)(2,1)S(1)}, bf16[256,1024]{1,0:T(8,128)(2,1)}, u32[]{:S(2)}, u32[]{:S(2)}) %collective-permute-start.8) | collective-permute-done | bytes 524320 | tf_op jit(solution)/shard_map/ppermute | solution.py:394
  102.0 1.7 collective-permute-start.9
  103.6 1.6 collective-permute-start.13
  105.2 12.0 %collective-permute-done.12 = bf16[512,1024]{1,0:T(8,128)(2,1)} collective-permute-done((bf16[512,1024]{1,0:T(8,128)(2,1)}, bf16[512,1024]{1,0:T(8,128)(2,1)}, u32[]{:S(2)}, u32[]{:S(2)}) %collective-permute-start.12) | collective-permute-done | bytes 1048608 | tf_op jit(solution)/shard_map/ppermute | solution.py:404
  118.7 2.2 collective-permute-start.11
  121.2 51.0 %collective-permute-done.11 = bf16[256,1024]{1,0:T(8,128)(2,1)} collective-permute-done((bf16[256,1024]{1,0:T(8,128)(2,1)}, bf16[256,1024]{1,0:T(8,128)(2,1)}, u32[]{:S(2)}, u32[]{:S(2)}) %collective-permute-start.11) | collective-permute-done | bytes 524320 | tf_op jit(solution)/shard_map/ppermute | solution.py:404
  175.4 5.2 %attention.1 = bf16[64,4096]{1,0:T(8,128)(2,1)S(1)} custom-call(bf16[32,544,128]{2,1,0:T(8,128)(2,1)} %all-to-all-done.5.message_ref, f32[32,128]{1,0:T(8,128)} %bitcast_convert_fusion.1.gain_ref, bf16[3,4096,128]{2,1,0:T(8,128)(2,1)} %wqkv_hbm.1, f32[32,128]{1,0:T(8,128)} %get-tuple-element.447.cos_ref, f32[32,128]{1,0:T(8,128)} %get-tuple-element.448.sin_ref, ...), custom_call_target="tpu_custom_call" | custom-call | flops 400000000 | bytes 9437184 | tf_op jit(solution)/shard_map/attention/pallas_call | solution.py:107
  183.8 58.4 %conditional.1 = (f32[32,40,128]{2,1,0:T(8,128)}) conditional(s32[]{:T(128)} %clamp.3, (s32[8]{0:T(128)S(1)}, bf16[8,4096,128]{2,1,0:T(8,128)(2,1)}, bf16[64,4096]{1,0:T(8,128)(2,1)S(1)}, s32[4]{0:T(128)S(1)}, bf16[32,544,128]{2,1,0:T(8,128)(2,1)}, /*index=5*/bf16[512,1024]{1,0:T(8,128)(2,1)}, ...), branch_computations={%region_1.2_spmd, %region_2.3_spmd, %region_3.4_spmd, %region_4.5_... | conditional | flops 17179969536 | bytes 76546120 | solution.py:495
  183.8 4.4 %branch_2_fun.1 = bf16[32,320,128]{2,1,0:T(8,128)(2,1)} custom-call(s32[8]{0:T(128)S(1)} %get-tuple-element.342.lens_ref, bf16[8,4096,128]{2,1,0:T(8,128)(2,1)} %get-tuple-element.343.pieces_ref, bf16[64,4096]{1,0:T(8,128)(2,1)S(1)} %get-tuple-element.344.refs_0_), custom_call_target="tpu_custom_call" | custom-call | bytes 5242880 | tf_op jit(solution)/shard_map/cond/branch_2_fun/pallas_call | solution.py:329
  188.2 6.7 %all-to-all-start.2 = ((bf16[32,320,128]{2,1,0:T(8,128)(2,1)}), bf16[32,320,128]{2,1,0:T(8,128)(2,1)}, u32[]{:S(2)}, u32[]{:S(2)}) async-start(bf16[32,320,128]{2,1,0:T(8,128)(2,1)} %branch_2_fun.1), calls=%async_computation.2 | async-start | bytes 5242880 | tf_op jit(solution)/shard_map/cond/branch_2_fun/all_to_all | solution.py:383
  195.0 16.6 %score.12.refs_0_ = f32[4,128]{1,0:T(4,128)} custom-call(s32[4]{0:T(128)S(1)} %get-tuple-element.345.place_ref, bf16[32,544,128]{2,1,0:T(8,128)(2,1)} %get-tuple-element.346.x_hbm, bf16[512,1024]{1,0:T(8,128)(2,1)} %get-tuple-element.347.refs_0_, bf16[512,1024]{1,0:T(8,128)(2,1)S(1)} %get-tuple-element.348.refs_1_, ...), custom_call_target="tpu_custom_call" | custom-call | flops 8589934592 | bytes 25165824 | tf_op jit(solution)/shard_map/cond/branch_2_fun/score/pallas_call | solution.py:236
  211.6 17.3 %all-to-all-done.2.x_hbm.message_ref = bf16[32,320,128]{2,1,0:T(8,128)(2,1)} async-done(((bf16[32,320,128]{2,1,0:T(8,128)(2,1)}), bf16[32,320,128]{2,1,0:T(8,128)(2,1)}, u32[]{:S(2)}, u32[]{:S(2)}) %all-to-all-start.2) | async-done | bytes 2621472 | tf_op jit(solution)/shard_map/cond/branch_2_fun/all_to_all | solution.py:383
  228.9 10.3 %score.13.refs_1_ = f32[2,128]{1,0:T(2,128)} custom-call(s32[4]{0:T(128)S(1)} %get-tuple-element.345.place_ref, bf16[32,320,128]{2,1,0:T(8,128)(2,1)} %all-to-all-done.2.x_hbm.message_ref, bf16[512,1024]{1,0:T(8,128)(2,1)} %get-tuple-element.347.refs_0_, bf16[512,1024]{1,0:T(8,128)(2,1)S(1)} %get-tuple-element.348.refs_1_, ...), custom_call_target="tpu_custom_call" | custom-call | flops 4294967296 | bytes 25165824 | tf_op jit(solution)/shard_map/cond/branch_2_fun/score/pallas_call | solution.py:236
  239.2 2.7 %combine.7 = f32[32,40,128]{2,1,0:T(8,128)} custom-call(bf16[32,320,128]{2,1,0:T(8,128)(2,1)} %all-to-all-done.2.x_hbm.message_ref, f32[4,128]{1,0:T(4,128)} %score.12.refs_0_, f32[2,128]{1,0:T(2,128)} %score.13.refs_1_), custom_call_target="tpu_custom_call" | custom-call | flops 100000 | bytes 524288 | tf_op jit(solution)/shard_map/cond/branch_2_fun/combine/pallas_call | solution.py:142
  242.2 7.5 %all-to-all-start.6 = ((f32[32,40,128]{2,1,0:T(8,128)}), f32[32,40,128]{2,1,0:T(8,128)S(1)}, u32[]{:S(2)}, u32[]{:S(2)}) async-start(f32[32,40,128]{2,1,0:T(8,128)} %get-tuple-element.449), calls=%async_computation.6 | async-start | bytes 1310720 | tf_op jit(solution)/shard_map/all_to_all | solution.py:383
  250.4 12.9 %all-to-all-done.6.result_ref = f32[32,40,128]{2,1,0:T(8,128)S(1)} async-done(((f32[32,40,128]{2,1,0:T(8,128)}), f32[32,40,128]{2,1,0:T(8,128)S(1)}, u32[]{:S(2)}, u32[]{:S(2)}) %all-to-all-start.6) | async-done | bytes 655392 | tf_op jit(solution)/shard_map/all_to_all | solution.py:383
  (80 shorter events, 14.5 us)
Async XLA Ops:
  2.3 8.5 %collective-permute-start = (bf16[128,1024]{1,0:T(8,128)(2,1)S(1)}, bf16[128,1024]{1,0:T(8,128)(2,1)S(1)}, u32[]{:S(2)}, u32[]{:S(2)}) collective-permute-start(bf16[128,1024]{1,0:T(8,128)(2,1)S(1)} %get-tuple-element.443), channel_id=1, source_target_pairs={{0,2},{2,4},{4,6},{6,0},{8,10},{10,12},{12,14},{14,8},{16,18},{18,... | collective-permute-start | bytes 786440 | tf_op jit(solution)/shard_map/ppermute | solution.py:394
  4.4 6.6 %collective-permute-start.1 = (bf16[128,1024]{1,0:T(8,128)(2,1)S(1)}, bf16[128,1024]{1,0:T(8,128)(2,1)S(1)}, u32[]{:S(2)}, u32[]{:S(2)}) collective-permute-start(bf16[128,1024]{1,0:T(8,128)(2,1)S(1)} %get-tuple-element.443), channel_id=1, source_target_pairs={{0,6},{2,0},{4,2},{6,4},{8,14},{10,8},{12,10},{14,12},{16,22},{18,... | collective-permute-start | bytes 786440 | tf_op jit(solution)/shard_map/ppermute | solution.py:394
  10.9 6.2 %collective-permute-start.2 = (bf16[64,1024]{1,0:T(8,128)(2,1)S(1)}, bf16[64,1024]{1,0:T(8,128)(2,1)S(1)}, u32[]{:S(2)}, u32[]{:S(2)}) collective-permute-start(bf16[64,1024]{1,0:T(8,128)(2,1)S(1)} %slice.20), channel_id=1, source_target_pairs={{0,2},{2,4},{4,6},{6,0},{8,10},{10,12},{12,14},{14,8},{16,18},{18,... | collective-permute-start | bytes 393224 | tf_op jit(solution)/shard_map/ppermute | solution.py:394
  11.0 6.8 %collective-permute-start.3 = (bf16[64,1024]{1,0:T(8,128)(2,1)S(1)}, bf16[64,1024]{1,0:T(8,128)(2,1)S(1)}, u32[]{:S(2)}, u32[]{:S(2)}) collective-permute-start(bf16[64,1024]{1,0:T(8,128)(2,1)S(1)} %slice.21), channel_id=1, source_target_pairs={{0,6},{2,0},{4,2},{6,4},{8,14},{10,8},{12,10},{14,12},{16,22},{18,... | collective-permute-start | bytes 393224 | tf_op jit(solution)/shard_map/ppermute | solution.py:394
  18.4 16.4 %collective-permute-start.4 = (bf16[512,1024]{1,0:T(8,128)(2,1)}, bf16[512,1024]{1,0:T(8,128)(2,1)S(1)}, u32[]{:S(2)}, u32[]{:S(2)}) collective-permute-start(bf16[512,1024]{1,0:T(8,128)(2,1)} %constant_dynamic-update-slice_fusion), channel_id=1, source_target_pairs={{0,8},{2,10},{4,12},{6,14},{8,16},{10,18},{12,20},{14,22},{16,24},... | collective-permute-start | bytes 3145736 | tf_op jit(solution)/shard_map/ppermute | solution.py:394
  19.9 15.1 %collective-permute-start.5 = (bf16[512,1024]{1,0:T(8,128)(2,1)}, bf16[512,1024]{1,0:T(8,128)(2,1)}, u32[]{:S(2)}, u32[]{:S(2)}) collective-permute-start(bf16[512,1024]{1,0:T(8,128)(2,1)} %constant_dynamic-update-slice_fusion), channel_id=1, source_target_pairs={{0,24},{2,26},{4,28},{6,30},{8,0},{10,2},{12,4},{14,6},{16,8},{18,... | collective-permute-start | bytes 3145736 | tf_op jit(solution)/shard_map/ppermute | solution.py:394
  23.6 1.2 collective-permute-start.6
  24.9 10.0 %collective-permute-start.7 = (f32[8,128]{1,0:T(8,128)S(1)}, f32[8,128]{1,0:T(8,128)S(1)}, u32[]{:S(2)}, u32[]{:S(2)}) collective-permute-start(f32[8,128]{1,0:T(8,128)S(1)} %broadcast_maximum_fusion), channel_id=1, source_target_pairs={{0,64},{64,0},{1,65},{65,1},{2,66},{66,2},{3,67},{67,3},{4,68},{68... | collective-permute-start | bytes 12296 | tf_op jit(solution)/shard_map/ppermute | solution.py:464
  36.9 84.0 %copy-start.13 = (s32[8]{0:T(128)S(1)}, s32[8]{0:T(128)}, u32[]{:S(2)}) copy-start(s32[8]{0:T(128)} %param.21) | copy-start | bytes 100
  36.9 137.2 %copy-start.9 = (bf16[4096]{0:T(1024)(128)(2,1)S(1)}, bf16[4096]{0:T(1024)(128)(2,1)}, u32[]{:S(2)}) copy-start(bf16[4096]{0:T(1024)(128)(2,1)} %param.23) | copy-start | bytes 24580
  36.9 137.8 %all-to-all-start.5 = ((bf16[32,544,128]{2,1,0:T(8,128)(2,1)}), bf16[32,544,128]{2,1,0:T(8,128)(2,1)}, u32[]{:S(2)}, u32[]{:S(2)}) async-start(bf16[32,544,128]{2,1,0:T(8,128)(2,1)} %shard_map.158), calls=%async_computation.5 | async-start | bytes 8912896 | tf_op jit(solution)/shard_map/all_to_all | solution.py:383
  44.9 72.2 %collective-permute-start.12 = (bf16[512,1024]{1,0:T(8,128)(2,1)}, bf16[512,1024]{1,0:T(8,128)(2,1)}, u32[]{:S(2)}, u32[]{:S(2)}) collective-permute-start(bf16[512,1024]{1,0:T(8,128)(2,1)} %constant_dynamic-update-slice_fusion), channel_id=1, source_target_pairs={{0,1},{1,0},{64,65},{65,64},{2,3},{3,2},{66,67},{67,66},{4,5},{5,4... | collective-permute-start | bytes 3145736 | tf_op jit(solution)/shard_map/ppermute | solution.py:404
  46.7 71.4 %collective-permute-start.15 = (bf16[512,1024]{1,0:T(8,128)(2,1)}, bf16[512,1024]{1,0:T(8,128)(2,1)}, u32[]{:S(2)}, u32[]{:S(2)}) collective-permute-start(bf16[512,1024]{1,0:T(8,128)(2,1)} %constant_dynamic-update-slice_fusion), channel_id=1, source_target_pairs={{0,32},{32,0},{1,33},{33,1},{2,34},{34,2},{3,35},{35,3},{4,36},{36... | collective-permute-start | bytes 3145736 | tf_op jit(solution)/shard_map/ppermute | solution.py:426
  46.7 55.2 %collective-permute-start.8 = (bf16[256,1024]{1,0:T(8,128)(2,1)S(1)}, bf16[256,1024]{1,0:T(8,128)(2,1)}, u32[]{:S(2)}, u32[]{:S(2)}) collective-permute-start(bf16[256,1024]{1,0:T(8,128)(2,1)S(1)} %slice.22), channel_id=1, source_target_pairs={{0,8},{2,10},{4,12},{6,14},{8,16},{10,18},{12,20},{14,22},{16,24},... | collective-permute-start | bytes 1572872 | tf_op jit(solution)/shard_map/ppermute | solution.py:394
  48.2 70.0 %collective-permute-start.10 = (bf16[256,1024]{1,0:T(8,128)(2,1)}, bf16[256,1024]{1,0:T(8,128)(2,1)}, u32[]{:S(2)}, u32[]{:S(2)}) collective-permute-start(bf16[256,1024]{1,0:T(8,128)(2,1)} %slice.23), channel_id=1, source_target_pairs={{0,24},{2,26},{4,28},{6,30},{8,0},{10,2},{12,4},{14,6},{16,8},{18,... | collective-permute-start | bytes 1572872 | tf_op jit(solution)/shard_map/ppermute | solution.py:394
  102.0 16.7 %collective-permute-start.9 = (bf16[256,1024]{1,0:T(8,128)(2,1)}, bf16[256,1024]{1,0:T(8,128)(2,1)S(1)}, u32[]{:S(2)}, u32[]{:S(2)}) collective-permute-start(bf16[256,1024]{1,0:T(8,128)(2,1)} %collective-permute-done.8), channel_id=1, source_target_pairs={{1,64},{64,1},{65,0},{0,65},{3,66},{66,3},{67,2},{2,67},{5,68},{68... | collective-permute-start | bytes 1572872 | tf_op jit(solution)/shard_map/ppermute | solution.py:404
  103.6 68.5 %collective-permute-start.13 = (bf16[512,1024]{1,0:T(8,128)(2,1)S(1)}, bf16[512,1024]{1,0:T(8,128)(2,1)}, u32[]{:S(2)}, u32[]{:S(2)}) collective-permute-start(bf16[512,1024]{1,0:T(8,128)(2,1)S(1)} %collective-permute-done.4), channel_id=1, source_target_pairs={{1,64},{64,1},{65,0},{0,65},{3,66},{66,3},{67,2},{2,67},{5,68},{68... | collective-permute-start | bytes 3145736 | tf_op jit(solution)/shard_map/ppermute | solution.py:404
  117.2 55.5 %collective-permute-start.14 = (bf16[512,1024]{1,0:T(8,128)(2,1)}, bf16[512,1024]{1,0:T(8,128)(2,1)}, u32[]{:S(2)}, u32[]{:S(2)}) collective-permute-start(bf16[512,1024]{1,0:T(8,128)(2,1)} %collective-permute-done.5), channel_id=1, source_target_pairs={{1,64},{64,1},{65,0},{0,65},{3,66},{66,3},{67,2},{2,67},{5,68},{68... | collective-permute-start | bytes 3145736 | tf_op jit(solution)/shard_map/ppermute | solution.py:404
  118.2 54.6 %collective-permute-start.16 = (bf16[512,1024]{1,0:T(8,128)(2,1)S(1)}, bf16[512,1024]{1,0:T(8,128)(2,1)S(1)}, u32[]{:S(2)}, u32[]{:S(2)}) collective-permute-start(bf16[512,1024]{1,0:T(8,128)(2,1)S(1)} %collective-permute-done.4), channel_id=1, source_target_pairs={{0,32},{32,0},{1,33},{33,1},{2,34},{34,2},{3,35},{35,3},{4,36},{36... | collective-permute-start | bytes 3145736 | tf_op jit(solution)/shard_map/ppermute | solution.py:426
  118.2 55.0 %collective-permute-start.17 = (bf16[512,1024]{1,0:T(8,128)(2,1)}, bf16[512,1024]{1,0:T(8,128)(2,1)}, u32[]{:S(2)}, u32[]{:S(2)}) collective-permute-start(bf16[512,1024]{1,0:T(8,128)(2,1)} %collective-permute-done.5), channel_id=1, source_target_pairs={{0,32},{32,0},{1,33},{33,1},{2,34},{34,2},{3,35},{35,3},{4,36},{36... | collective-permute-start | bytes 3145736 | tf_op jit(solution)/shard_map/ppermute | solution.py:426
  118.7 56.7 %copy-start.3 = (bf16[256,1024]{1,0:T(8,128)(2,1)}, bf16[256,1024]{1,0:T(8,128)(2,1)S(1)}, u32[]{:S(2)}) copy-start(bf16[256,1024]{1,0:T(8,128)(2,1)S(1)} %collective-permute-done.9) | copy-start | bytes 1572868
  118.7 53.5 %collective-permute-start.11 = (bf16[256,1024]{1,0:T(8,128)(2,1)}, bf16[256,1024]{1,0:T(8,128)(2,1)}, u32[]{:S(2)}, u32[]{:S(2)}) collective-permute-start(bf16[256,1024]{1,0:T(8,128)(2,1)} %collective-permute-done.10), channel_id=1, source_target_pairs={{1,64},{64,1},{65,0},{0,65},{3,66},{66,3},{67,2},{2,67},{5,68},{68... | collective-permute-start | bytes 1572872 | tf_op jit(solution)/shard_map/ppermute | solution.py:404
  172.2 10.4 %collective-permute-start.20 = (bf16[512,1024]{1,0:T(8,128)(2,1)}, bf16[512,1024]{1,0:T(8,128)(2,1)}, u32[]{:S(2)}, u32[]{:S(2)}) collective-permute-start(bf16[512,1024]{1,0:T(8,128)(2,1)} %collective-permute-done.12), channel_id=1, source_target_pairs={{0,32},{32,0},{1,33},{33,1},{2,34},{34,2},{3,35},{35,3},{4,36},{36... | collective-permute-start | bytes 3145736 | tf_op jit(solution)/shard_map/ppermute | solution.py:426
  172.2 8.5 %collective-permute-start.18 = (bf16[256,1024]{1,0:T(8,128)(2,1)}, bf16[256,1024]{1,0:T(8,128)(2,1)}, u32[]{:S(2)}, u32[]{:S(2)}) collective-permute-start(bf16[256,1024]{1,0:T(8,128)(2,1)} %collective-permute-done.8), channel_id=1, source_target_pairs={{0,32},{32,0},{1,33},{33,1},{2,34},{34,2},{3,35},{35,3},{4,36},{36... | collective-permute-start | bytes 1572872 | tf_op jit(solution)/shard_map/ppermute | solution.py:426
  172.7 8.5 %collective-permute-start.19 = (bf16[256,1024]{1,0:T(8,128)(2,1)}, bf16[256,1024]{1,0:T(8,128)(2,1)}, u32[]{:S(2)}, u32[]{:S(2)}) collective-permute-start(bf16[256,1024]{1,0:T(8,128)(2,1)} %collective-permute-done.10), channel_id=1, source_target_pairs={{0,32},{32,0},{1,33},{33,1},{2,34},{34,2},{3,35},{35,3},{4,36},{36... | collective-permute-start | bytes 1572872 | tf_op jit(solution)/shard_map/ppermute | solution.py:426
  172.8 9.8 %collective-permute-start.21 = (bf16[512,1024]{1,0:T(8,128)(2,1)}, bf16[512,1024]{1,0:T(8,128)(2,1)}, u32[]{:S(2)}, u32[]{:S(2)}) collective-permute-start(bf16[512,1024]{1,0:T(8,128)(2,1)} %collective-permute-done.13), channel_id=1, source_target_pairs={{0,32},{32,0},{1,33},{33,1},{2,34},{34,2},{3,35},{35,3},{4,36},{36... | collective-permute-start | bytes 3145736 | tf_op jit(solution)/shard_map/ppermute | solution.py:426
  173.2 9.4 %collective-permute-start.22 = (bf16[512,1024]{1,0:T(8,128)(2,1)}, bf16[512,1024]{1,0:T(8,128)(2,1)}, u32[]{:S(2)}, u32[]{:S(2)}) collective-permute-start(bf16[512,1024]{1,0:T(8,128)(2,1)} %collective-permute-done.14), channel_id=1, source_target_pairs={{0,32},{32,0},{1,33},{33,1},{2,34},{34,2},{3,35},{35,3},{4,36},{36... | collective-permute-start | bytes 3145736 | tf_op jit(solution)/shard_map/ppermute | solution.py:426
  175.4 8.3 %copy-start.8 = (s32[8]{0:T(128)S(1)}, s32[8]{0:T(128)}, u32[]{:S(2)}) copy-start(s32[8]{0:T(128)} %lens_ref.1) | copy-start | bytes 100
  180.6 2.4 collective-permute-start.23
  181.1 2.6 collective-permute-start.24
  188.2 40.7 %all-to-all-start.2 = ((bf16[32,320,128]{2,1,0:T(8,128)(2,1)}), bf16[32,320,128]{2,1,0:T(8,128)(2,1)}, u32[]{:S(2)}, u32[]{:S(2)}) async-start(bf16[32,320,128]{2,1,0:T(8,128)(2,1)} %branch_2_fun.1), calls=%async_computation.2 | async-start | bytes 5242880 | tf_op jit(solution)/shard_map/cond/branch_2_fun/all_to_all | solution.py:383
  242.2 21.1 %all-to-all-start.6 = ((f32[32,40,128]{2,1,0:T(8,128)}), f32[32,40,128]{2,1,0:T(8,128)S(1)}, u32[]{:S(2)}, u32[]{:S(2)}) async-start(f32[32,40,128]{2,1,0:T(8,128)} %get-tuple-element.449), calls=%async_computation.6 | async-start | bytes 1310720 | tf_op jit(solution)/shard_map/all_to_all | solution.py:383
  (5 other events, 27.0 us)

commit v2 on v1

--- a/solution.py
+++ b/solution.py
@@ -396,8 +396,10 @@
 
 def around(value, stage):
     half = value.shape[0] // 2
-    right, left = shift(value, stage, 1), shift(value, stage, -1)
-    return (value, right, left, shift(right[:half], stage, 1), shift(left[half:], stage, -1))
+    right = shift(value, stage, 1)
+    left = shift(value, stage, -1)
+    ahead = shift(right[:half], stage, 1)
+    return (value, right, left, ahead, shift(left[half:], stage, -1))
 
 
 def across(value, pairs):
@@ -409,7 +411,8 @@
     own = lax.dynamic_slice_in_dim(w_value, lax.axis_index("core") * columns, columns, axis=1)
     plane = jnp.concatenate(around(own, 0), axis=0)
     half = plane.shape[0] // 2
-    right, left = shift(plane, 1, 1), shift(plane, 1, -1)
+    right = shift(plane, 1, 1)
+    left = shift(plane, 1, -1)
     ahead, behind, message, most = lax.optimization_barrier((right[:half], left[half:], message, most))
     near = (plane, right, left)
     ahead = shift(ahead, 1, 1)

time: 266 us -> 266 us (level)
  no operation moved by 1% of the time
where the time goes in v2:
time: 266 us; the launch traced here: 265 us
  waiting for transfers between devices  153 us (58%)
  starting transfers between devices  49.9 us (19%)
  Pallas kernels  45.9 us (17%)
  local copies, waits for them, and re-layouts  9.28 us (3%)
  other arithmetic  2.92 us (1%)
  between operations  2.85 us (1%)
    ppermute x5, waiting for transfers between devices, across(): lax.ppermute(value, ('yhi', 'ylo'), [pair for i, j in pairs for pair in (...  62.9 us
    ppermute x8, waiting for transfers between devices, shift(): return lax.ppermute(value, ('core', 'x', 'z'), pairs)  57.8 us
    all_to_all x3, waiting for transfers between devices, exchange(): return lax.all_to_all(message, MP, 0, 0)  30.2 us
    pallas_call x2, Pallas kernels, score_rows(): pl.pallas_call(functools.partial(score_kernel, slots), out_shape=jax.Shap...  26.9 us
    all_to_all x3, starting transfers between devices, exchange(): return lax.all_to_all(message, MP, 0, 0)  22.2 us
    ppermute x8, starting transfers between devices, shift(): return lax.ppermute(value, ('core', 'x', 'z'), pairs)  14 us
    pallas_call x2, Pallas kernels, pack(): pl.pallas_call(functools.partial(pack_kernel, operands[1].shape[0], first...  9.81 us
    ppermute x5, starting transfers between devices, across(): lax.ppermute(value, ('yhi', 'ylo'), [pair for i, j in pairs for pair in (...  8.28 us
  transfers between devices with their start and end apart: 28, of which 11 were waited for; matrix products, arithmetic and copies ran while one was open for 3% of the time, Pallas kernels for 10%

profile of v2, /device:TPU:0, one launch (start us, length us, event | category | flops | bytes accessed | tf_op | source)
XLA Modules:
  0.0 264.6 jit_solution(10413377055577844097)
XLA Ops:
  0.6 1.7 constant_dynamic-update-slice_fusion.4
  2.3 2.0 collective-permute-start
  4.4 2.1 collective-permute-start.1
  6.5 4.3 %collective-permute-done = bf16[128,1024]{1,0:T(8,128)(2,1)S(1)} collective-permute-done((bf16[128,1024]{1,0:T(8,128)(2,1)S(1)}, bf16[128,1024]{1,0:T(8,128)(2,1)S(1)}, u32[]{:S(2)}, u32[]{:S(2)}) %collective-permute-start) | collective-permute-done | bytes 262176 | tf_op jit(solution)/shard_map/ppermute | solution.py:394
  11.0 3.3 %collective-permute-start.3 = (bf16[64,1024]{1,0:T(8,128)(2,1)S(1)}, bf16[64,1024]{1,0:T(8,128)(2,1)S(1)}, u32[]{:S(2)}, u32[]{:S(2)}) collective-permute-start(bf16[64,1024]{1,0:T(8,128)(2,1)S(1)} %slice.21), channel_id=1, source_target_pairs={{0,6},{2,0},{4,2},{6,4},{8,14},{10,8},{12,10},{14,12},{16,22},{18,... | collective-permute-start | bytes 393224 | tf_op jit(solution)/shard_map/ppermute | solution.py:394
  15.7 1.4 collective-permute-done.2
  18.4 1.5 collective-permute-start.4
  19.9 1.7 collective-permute-start.5
  24.9 3.2 %collective-permute-start.7 = (f32[8,128]{1,0:T(8,128)S(1)}, f32[8,128]{1,0:T(8,128)S(1)}, u32[]{:S(2)}, u32[]{:S(2)}) collective-permute-start(f32[8,128]{1,0:T(8,128)S(1)} %broadcast_maximum_fusion), channel_id=1, source_target_pairs={{0,64},{64,0},{1,65},{65,1},{2,66},{66,2},{3,67},{67,3},{4,68},{68... | collective-permute-start | bytes 12296 | tf_op jit(solution)/shard_map/ppermute | solution.py:467
  28.1 1.3 copy.18.refs_0_
  29.4 5.4 %shard_map.158 = bf16[32,544,128]{2,1,0:T(8,128)(2,1)} custom-call(s32[8]{0:T(128)} %lens_ref.1, bf16[8,4096,128]{2,1,0:T(8,128)(2,1)} %pieces_ref.1, s32[8,4]{1,0:T(8,128)} %copy.18.refs_0_, bf16[32000,128]{1,0:T(8,128)(2,1)} %refs_1_.1), custom_call_target="tpu_custom_call" | custom-call | bytes 8912896 | tf_op jit(solution)/shard_map/pallas_call | solution.py:329
  35.0 1.9 slice.23
  36.9 8.0 %all-to-all-start.5 = ((bf16[32,544,128]{2,1,0:T(8,128)(2,1)}), bf16[32,544,128]{2,1,0:T(8,128)(2,1)}, u32[]{:S(2)}, u32[]{:S(2)}) async-start(bf16[32,544,128]{2,1,0:T(8,128)(2,1)} %shard_map.158), calls=%async_computation.5 | async-start | bytes 8912896 | tf_op jit(solution)/shard_map/all_to_all | solution.py:383
  44.9 1.8 collective-permute-start.12
  46.7 1.5 collective-permute-start.8
  48.2 1.8 collective-permute-start.10
  50.0 52.0 %collective-permute-done.8 = bf16[256,1024]{1,0:T(8,128)(2,1)} collective-permute-done((bf16[256,1024]{1,0:T(8,128)(2,1)S(1)}, bf16[256,1024]{1,0:T(8,128)(2,1)}, u32[]{:S(2)}, u32[]{:S(2)}) %collective-permute-start.8) | collective-permute-done | bytes 524320 | tf_op jit(solution)/shard_map/ppermute | solution.py:394
  102.0 1.7 collective-permute-start.9
  103.6 1.6 collective-permute-start.13
  105.2 12.0 %collective-permute-done.12 = bf16[512,1024]{1,0:T(8,128)(2,1)} collective-permute-done((bf16[512,1024]{1,0:T(8,128)(2,1)}, bf16[512,1024]{1,0:T(8,128)(2,1)}, u32[]{:S(2)}, u32[]{:S(2)}) %collective-permute-start.12) | collective-permute-done | bytes 1048608 | tf_op jit(solution)/shard_map/ppermute | solution.py:406
  118.7 2.2 collective-permute-start.11
  121.2 51.0 %collective-permute-done.11 = bf16[256,1024]{1,0:T(8,128)(2,1)} collective-permute-done((bf16[256,1024]{1,0:T(8,128)(2,1)}, bf16[256,1024]{1,0:T(8,128)(2,1)}, u32[]{:S(2)}, u32[]{:S(2)}) %collective-permute-start.11) | collective-permute-done | bytes 524320 | tf_op jit(solution)/shard_map/ppermute | solution.py:406
  175.4 5.2 %attention.1 = bf16[64,4096]{1,0:T(8,128)(2,1)S(1)} custom-call(bf16[32,544,128]{2,1,0:T(8,128)(2,1)} %all-to-all-done.5.message_ref, f32[32,128]{1,0:T(8,128)} %bitcast_convert_fusion.1.gain_ref, bf16[3,4096,128]{2,1,0:T(8,128)(2,1)} %wqkv_hbm.1, f32[32,128]{1,0:T(8,128)} %get-tuple-element.447.cos_ref, f32[32,128]{1,0:T(8,128)} %get-tuple-element.448.sin_ref, ...), custom_call_target="tpu_custom_call" | custom-call | flops 400000000 | bytes 9437184 | tf_op jit(solution)/shard_map/attention/pallas_call | solution.py:107
  183.8 58.4 %conditional.1 = (f32[32,40,128]{2,1,0:T(8,128)}) conditional(s32[]{:T(128)} %clamp.3, (s32[8]{0:T(128)S(1)}, bf16[8,4096,128]{2,1,0:T(8,128)(2,1)}, bf16[64,4096]{1,0:T(8,128)(2,1)S(1)}, s32[4]{0:T(128)S(1)}, bf16[32,544,128]{2,1,0:T(8,128)(2,1)}, /*index=5*/bf16[512,1024]{1,0:T(8,128)(2,1)}, ...), branch_computations={%region_1.2_spmd, %region_2.3_spmd, %region_3.4_spmd, %region_4.5_... | conditional | flops 17179969536 | bytes 76546120 | solution.py:498
  183.8 4.4 %branch_2_fun.1 = bf16[32,320,128]{2,1,0:T(8,128)(2,1)} custom-call(s32[8]{0:T(128)S(1)} %get-tuple-element.342.lens_ref, bf16[8,4096,128]{2,1,0:T(8,128)(2,1)} %get-tuple-element.343.pieces_ref, bf16[64,4096]{1,0:T(8,128)(2,1)S(1)} %get-tuple-element.344.refs_0_), custom_call_target="tpu_custom_call" | custom-call | bytes 5242880 | tf_op jit(solution)/shard_map/cond/branch_2_fun/pallas_call | solution.py:329
  188.2 6.7 %all-to-all-start.2 = ((bf16[32,320,128]{2,1,0:T(8,128)(2,1)}), bf16[32,320,128]{2,1,0:T(8,128)(2,1)}, u32[]{:S(2)}, u32[]{:S(2)}) async-start(bf16[32,320,128]{2,1,0:T(8,128)(2,1)} %branch_2_fun.1), calls=%async_computation.2 | async-start | bytes 5242880 | tf_op jit(solution)/shard_map/cond/branch_2_fun/all_to_all | solution.py:383
  195.0 16.6 %score.12.refs_0_ = f32[4,128]{1,0:T(4,128)} custom-call(s32[4]{0:T(128)S(1)} %get-tuple-element.345.place_ref, bf16[32,544,128]{2,1,0:T(8,128)(2,1)} %get-tuple-element.346.x_hbm, bf16[512,1024]{1,0:T(8,128)(2,1)} %get-tuple-element.347.refs_0_, bf16[512,1024]{1,0:T(8,128)(2,1)S(1)} %get-tuple-element.348.refs_1_, ...), custom_call_target="tpu_custom_call" | custom-call | flops 8589934592 | bytes 25165824 | tf_op jit(solution)/shard_map/cond/branch_2_fun/score/pallas_call | solution.py:236
  211.6 17.3 %all-to-all-done.2.x_hbm.message_ref = bf16[32,320,128]{2,1,0:T(8,128)(2,1)} async-done(((bf16[32,320,128]{2,1,0:T(8,128)(2,1)}), bf16[32,320,128]{2,1,0:T(8,128)(2,1)}, u32[]{:S(2)}, u32[]{:S(2)}) %all-to-all-start.2) | async-done | bytes 2621472 | tf_op jit(solution)/shard_map/cond/branch_2_fun/all_to_all | solution.py:383
  228.9 10.3 %score.13.refs_1_ = f32[2,128]{1,0:T(2,128)} custom-call(s32[4]{0:T(128)S(1)} %get-tuple-element.345.place_ref, bf16[32,320,128]{2,1,0:T(8,128)(2,1)} %all-to-all-done.2.x_hbm.message_ref, bf16[512,1024]{1,0:T(8,128)(2,1)} %get-tuple-element.347.refs_0_, bf16[512,1024]{1,0:T(8,128)(2,1)S(1)} %get-tuple-element.348.refs_1_, ...), custom_call_target="tpu_custom_call" | custom-call | flops 4294967296 | bytes 25165824 | tf_op jit(solution)/shard_map/cond/branch_2_fun/score/pallas_call | solution.py:236
  239.2 2.7 %combine.7 = f32[32,40,128]{2,1,0:T(8,128)} custom-call(bf16[32,320,128]{2,1,0:T(8,128)(2,1)} %all-to-all-done.2.x_hbm.message_ref, f32[4,128]{1,0:T(4,128)} %score.12.refs_0_, f32[2,128]{1,0:T(2,128)} %score.13.refs_1_), custom_call_target="tpu_custom_call" | custom-call | flops 100000 | bytes 524288 | tf_op jit(solution)/shard_map/cond/branch_2_fun/combine/pallas_call | solution.py:142
  242.2 7.5 %all-to-all-start.6 = ((f32[32,40,128]{2,1,0:T(8,128)}), f32[32,40,128]{2,1,0:T(8,128)S(1)}, u32[]{:S(2)}, u32[]{:S(2)}) async-start(f32[32,40,128]{2,1,0:T(8,128)} %get-tuple-element.449), calls=%async_computation.6 | async-start | bytes 1310720 | tf_op jit(solution)/shard_map/all_to_all | solution.py:383
  250.4 12.9 %all-to-all-done.6.result_ref = f32[32,40,128]{2,1,0:T(8,128)S(1)} async-done(((f32[32,40,128]{2,1,0:T(8,128)}), f32[32,40,128]{2,1,0:T(8,128)S(1)}, u32[]{:S(2)}, u32[]{:S(2)}) %all-to-all-start.6) | async-done | bytes 655392 | tf_op jit(solution)/shard_map/all_to_all | solution.py:383
  (80 shorter events, 14.5 us)
Async XLA Ops:
  2.3 8.5 %collective-permute-start = (bf16[128,1024]{1,0:T(8,128)(2,1)S(1)}, bf16[128,1024]{1,0:T(8,128)(2,1)S(1)}, u32[]{:S(2)}, u32[]{:S(2)}) collective-permute-start(bf16[128,1024]{1,0:T(8,128)(2,1)S(1)} %get-tuple-element.443), channel_id=1, source_target_pairs={{0,2},{2,4},{4,6},{6,0},{8,10},{10,12},{12,14},{14,8},{16,18},{18,... | collective-permute-start | bytes 786440 | tf_op jit(solution)/shard_map/ppermute | solution.py:394
  4.4 6.6 %collective-permute-start.1 = (bf16[128,1024]{1,0:T(8,128)(2,1)S(1)}, bf16[128,1024]{1,0:T(8,128)(2,1)S(1)}, u32[]{:S(2)}, u32[]{:S(2)}) collective-permute-start(bf16[128,1024]{1,0:T(8,128)(2,1)S(1)} %get-tuple-element.443), channel_id=1, source_target_pairs={{0,6},{2,0},{4,2},{6,4},{8,14},{10,8},{12,10},{14,12},{16,22},{18,... | collective-permute-start | bytes 786440 | tf_op jit(solution)/shard_map/ppermute | solution.py:394
  10.9 6.2 %collective-permute-start.2 = (bf16[64,1024]{1,0:T(8,128)(2,1)S(1)}, bf16[64,1024]{1,0:T(8,128)(2,1)S(1)}, u32[]{:S(2)}, u32[]{:S(2)}) collective-permute-start(bf16[64,1024]{1,0:T(8,128)(2,1)S(1)} %slice.20), channel_id=1, source_target_pairs={{0,2},{2,4},{4,6},{6,0},{8,10},{10,12},{12,14},{14,8},{16,18},{18,... | collective-permute-start | bytes 393224 | tf_op jit(solution)/shard_map/ppermute | solution.py:394
  11.0 6.8 %collective-permute-start.3 = (bf16[64,1024]{1,0:T(8,128)(2,1)S(1)}, bf16[64,1024]{1,0:T(8,128)(2,1)S(1)}, u32[]{:S(2)}, u32[]{:S(2)}) collective-permute-start(bf16[64,1024]{1,0:T(8,128)(2,1)S(1)} %slice.21), channel_id=1, source_target_pairs={{0,6},{2,0},{4,2},{6,4},{8,14},{10,8},{12,10},{14,12},{16,22},{18,... | collective-permute-start | bytes 393224 | tf_op jit(solution)/shard_map/ppermute | solution.py:394
  18.4 16.4 %collective-permute-start.4 = (bf16[512,1024]{1,0:T(8,128)(2,1)}, bf16[512,1024]{1,0:T(8,128)(2,1)S(1)}, u32[]{:S(2)}, u32[]{:S(2)}) collective-permute-start(bf16[512,1024]{1,0:T(8,128)(2,1)} %constant_dynamic-update-slice_fusion), channel_id=1, source_target_pairs={{0,8},{2,10},{4,12},{6,14},{8,16},{10,18},{12,20},{14,22},{16,24},... | collective-permute-start | bytes 3145736 | tf_op jit(solution)/shard_map/ppermute | solution.py:394
  19.9 15.1 %collective-permute-start.5 = (bf16[512,1024]{1,0:T(8,128)(2,1)}, bf16[512,1024]{1,0:T(8,128)(2,1)}, u32[]{:S(2)}, u32[]{:S(2)}) collective-permute-start(bf16[512,1024]{1,0:T(8,128)(2,1)} %constant_dynamic-update-slice_fusion), channel_id=1, source_target_pairs={{0,24},{2,26},{4,28},{6,30},{8,0},{10,2},{12,4},{14,6},{16,8},{18,... | collective-permute-start | bytes 3145736 | tf_op jit(solution)/shard_map/ppermute | solution.py:394
  23.6 1.2 collective-permute-start.6
  24.9 10.0 %collective-permute-start.7 = (f32[8,128]{1,0:T(8,128)S(1)}, f32[8,128]{1,0:T(8,128)S(1)}, u32[]{:S(2)}, u32[]{:S(2)}) collective-permute-start(f32[8,128]{1,0:T(8,128)S(1)} %broadcast_maximum_fusion), channel_id=1, source_target_pairs={{0,64},{64,0},{1,65},{65,1},{2,66},{66,2},{3,67},{67,3},{4,68},{68... | collective-permute-start | bytes 12296 | tf_op jit(solution)/shard_map/ppermute | solution.py:467
  36.9 84.0 %copy-start.13 = (s32[8]{0:T(128)S(1)}, s32[8]{0:T(128)}, u32[]{:S(2)}) copy-start(s32[8]{0:T(128)} %param.21) | copy-start | bytes 100
  36.9 137.2 %copy-start.9 = (bf16[4096]{0:T(1024)(128)(2,1)S(1)}, bf16[4096]{0:T(1024)(128)(2,1)}, u32[]{:S(2)}) copy-start(bf16[4096]{0:T(1024)(128)(2,1)} %param.23) | copy-start | bytes 24580
  36.9 137.8 %all-to-all-start.5 = ((bf16[32,544,128]{2,1,0:T(8,128)(2,1)}), bf16[32,544,128]{2,1,0:T(8,128)(2,1)}, u32[]{:S(2)}, u32[]{:S(2)}) async-start(bf16[32,544,128]{2,1,0:T(8,128)(2,1)} %shard_map.158), calls=%async_computation.5 | async-start | bytes 8912896 | tf_op jit(solution)/shard_map/all_to_all | solution.py:383
  44.9 72.2 %collective-permute-start.12 = (bf16[512,1024]{1,0:T(8,128)(2,1)}, bf16[512,1024]{1,0:T(8,128)(2,1)}, u32[]{:S(2)}, u32[]{:S(2)}) collective-permute-start(bf16[512,1024]{1,0:T(8,128)(2,1)} %constant_dynamic-update-slice_fusion), channel_id=1, source_target_pairs={{0,1},{1,0},{64,65},{65,64},{2,3},{3,2},{66,67},{67,66},{4,5},{5,4... | collective-permute-start | bytes 3145736 | tf_op jit(solution)/shard_map/ppermute | solution.py:406
  46.7 71.4 %collective-permute-start.15 = (bf16[512,1024]{1,0:T(8,128)(2,1)}, bf16[512,1024]{1,0:T(8,128)(2,1)}, u32[]{:S(2)}, u32[]{:S(2)}) collective-permute-start(bf16[512,1024]{1,0:T(8,128)(2,1)} %constant_dynamic-update-slice_fusion), channel_id=1, source_target_pairs={{0,32},{32,0},{1,33},{33,1},{2,34},{34,2},{3,35},{35,3},{4,36},{36... | collective-permute-start | bytes 3145736 | tf_op jit(solution)/shard_map/ppermute | solution.py:429
  46.7 55.2 %collective-permute-start.8 = (bf16[256,1024]{1,0:T(8,128)(2,1)S(1)}, bf16[256,1024]{1,0:T(8,128)(2,1)}, u32[]{:S(2)}, u32[]{:S(2)}) collective-permute-start(bf16[256,1024]{1,0:T(8,128)(2,1)S(1)} %slice.22), channel_id=1, source_target_pairs={{0,8},{2,10},{4,12},{6,14},{8,16},{10,18},{12,20},{14,22},{16,24},... | collective-permute-start | bytes 1572872 | tf_op jit(solution)/shard_map/ppermute | solution.py:394
  48.2 70.0 %collective-permute-start.10 = (bf16[256,1024]{1,0:T(8,128)(2,1)}, bf16[256,1024]{1,0:T(8,128)(2,1)}, u32[]{:S(2)}, u32[]{:S(2)}) collective-permute-start(bf16[256,1024]{1,0:T(8,128)(2,1)} %slice.23), channel_id=1, source_target_pairs={{0,24},{2,26},{4,28},{6,30},{8,0},{10,2},{12,4},{14,6},{16,8},{18,... | collective-permute-start | bytes 1572872 | tf_op jit(solution)/shard_map/ppermute | solution.py:394
  102.0 16.7 %collective-permute-start.9 = (bf16[256,1024]{1,0:T(8,128)(2,1)}, bf16[256,1024]{1,0:T(8,128)(2,1)S(1)}, u32[]{:S(2)}, u32[]{:S(2)}) collective-permute-start(bf16[256,1024]{1,0:T(8,128)(2,1)} %collective-permute-done.8), channel_id=1, source_target_pairs={{1,64},{64,1},{65,0},{0,65},{3,66},{66,3},{67,2},{2,67},{5,68},{68... | collective-permute-start | bytes 1572872 | tf_op jit(solution)/shard_map/ppermute | solution.py:406
  103.6 68.5 %collective-permute-start.13 = (bf16[512,1024]{1,0:T(8,128)(2,1)S(1)}, bf16[512,1024]{1,0:T(8,128)(2,1)}, u32[]{:S(2)}, u32[]{:S(2)}) collective-permute-start(bf16[512,1024]{1,0:T(8,128)(2,1)S(1)} %collective-permute-done.4), channel_id=1, source_target_pairs={{1,64},{64,1},{65,0},{0,65},{3,66},{66,3},{67,2},{2,67},{5,68},{68... | collective-permute-start | bytes 3145736 | tf_op jit(solution)/shard_map/ppermute | solution.py:406
  117.2 55.5 %collective-permute-start.14 = (bf16[512,1024]{1,0:T(8,128)(2,1)}, bf16[512,1024]{1,0:T(8,128)(2,1)}, u32[]{:S(2)}, u32[]{:S(2)}) collective-permute-start(bf16[512,1024]{1,0:T(8,128)(2,1)} %collective-permute-done.5), channel_id=1, source_target_pairs={{1,64},{64,1},{65,0},{0,65},{3,66},{66,3},{67,2},{2,67},{5,68},{68... | collective-permute-start | bytes 3145736 | tf_op jit(solution)/shard_map/ppermute | solution.py:406
  118.2 54.6 %collective-permute-start.16 = (bf16[512,1024]{1,0:T(8,128)(2,1)S(1)}, bf16[512,1024]{1,0:T(8,128)(2,1)S(1)}, u32[]{:S(2)}, u32[]{:S(2)}) collective-permute-start(bf16[512,1024]{1,0:T(8,128)(2,1)S(1)} %collective-permute-done.4), channel_id=1, source_target_pairs={{0,32},{32,0},{1,33},{33,1},{2,34},{34,2},{3,35},{35,3},{4,36},{36... | collective-permute-start | bytes 3145736 | tf_op jit(solution)/shard_map/ppermute | solution.py:429
  118.2 55.0 %collective-permute-start.17 = (bf16[512,1024]{1,0:T(8,128)(2,1)}, bf16[512,1024]{1,0:T(8,128)(2,1)}, u32[]{:S(2)}, u32[]{:S(2)}) collective-permute-start(bf16[512,1024]{1,0:T(8,128)(2,1)} %collective-permute-done.5), channel_id=1, source_target_pairs={{0,32},{32,0},{1,33},{33,1},{2,34},{34,2},{3,35},{35,3},{4,36},{36... | collective-permute-start | bytes 3145736 | tf_op jit(solution)/shard_map/ppermute | solution.py:429
  118.7 56.7 %copy-start.3 = (bf16[256,1024]{1,0:T(8,128)(2,1)}, bf16[256,1024]{1,0:T(8,128)(2,1)S(1)}, u32[]{:S(2)}) copy-start(bf16[256,1024]{1,0:T(8,128)(2,1)S(1)} %collective-permute-done.9) | copy-start | bytes 1572868
  118.7 53.5 %collective-permute-start.11 = (bf16[256,1024]{1,0:T(8,128)(2,1)}, bf16[256,1024]{1,0:T(8,128)(2,1)}, u32[]{:S(2)}, u32[]{:S(2)}) collective-permute-start(bf16[256,1024]{1,0:T(8,128)(2,1)} %collective-permute-done.10), channel_id=1, source_target_pairs={{1,64},{64,1},{65,0},{0,65},{3,66},{66,3},{67,2},{2,67},{5,68},{68... | collective-permute-start | bytes 1572872 | tf_op jit(solution)/shard_map/ppermute | solution.py:406
  172.2 10.4 %collective-permute-start.20 = (bf16[512,1024]{1,0:T(8,128)(2,1)}, bf16[512,1024]{1,0:T(8,128)(2,1)}, u32[]{:S(2)}, u32[]{:S(2)}) collective-permute-start(bf16[512,1024]{1,0:T(8,128)(2,1)} %collective-permute-done.12), channel_id=1, source_target_pairs={{0,32},{32,0},{1,33},{33,1},{2,34},{34,2},{3,35},{35,3},{4,36},{36... | collective-permute-start | bytes 3145736 | tf_op jit(solution)/shard_map/ppermute | solution.py:429
  172.2 8.5 %collective-permute-start.18 = (bf16[256,1024]{1,0:T(8,128)(2,1)}, bf16[256,1024]{1,0:T(8,128)(2,1)}, u32[]{:S(2)}, u32[]{:S(2)}) collective-permute-start(bf16[256,1024]{1,0:T(8,128)(2,1)} %collective-permute-done.8), channel_id=1, source_target_pairs={{0,32},{32,0},{1,33},{33,1},{2,34},{34,2},{3,35},{35,3},{4,36},{36... | collective-permute-start | bytes 1572872 | tf_op jit(solution)/shard_map/ppermute | solution.py:429
  172.7 8.5 %collective-permute-start.19 = (bf16[256,1024]{1,0:T(8,128)(2,1)}, bf16[256,1024]{1,0:T(8,128)(2,1)}, u32[]{:S(2)}, u32[]{:S(2)}) collective-permute-start(bf16[256,1024]{1,0:T(8,128)(2,1)} %collective-permute-done.10), channel_id=1, source_target_pairs={{0,32},{32,0},{1,33},{33,1},{2,34},{34,2},{3,35},{35,3},{4,36},{36... | collective-permute-start | bytes 1572872 | tf_op jit(solution)/shard_map/ppermute | solution.py:429
  172.8 9.8 %collective-permute-start.21 = (bf16[512,1024]{1,0:T(8,128)(2,1)}, bf16[512,1024]{1,0:T(8,128)(2,1)}, u32[]{:S(2)}, u32[]{:S(2)}) collective-permute-start(bf16[512,1024]{1,0:T(8,128)(2,1)} %collective-permute-done.13), channel_id=1, source_target_pairs={{0,32},{32,0},{1,33},{33,1},{2,34},{34,2},{3,35},{35,3},{4,36},{36... | collective-permute-start | bytes 3145736 | tf_op jit(solution)/shard_map/ppermute | solution.py:429
  173.2 9.4 %collective-permute-start.22 = (bf16[512,1024]{1,0:T(8,128)(2,1)}, bf16[512,1024]{1,0:T(8,128)(2,1)}, u32[]{:S(2)}, u32[]{:S(2)}) collective-permute-start(bf16[512,1024]{1,0:T(8,128)(2,1)} %collective-permute-done.14), channel_id=1, source_target_pairs={{0,32},{32,0},{1,33},{33,1},{2,34},{34,2},{3,35},{35,3},{4,36},{36... | collective-permute-start | bytes 3145736 | tf_op jit(solution)/shard_map/ppermute | solution.py:429
  175.4 8.3 %copy-start.8 = (s32[8]{0:T(128)S(1)}, s32[8]{0:T(128)}, u32[]{:S(2)}) copy-start(s32[8]{0:T(128)} %lens_ref.1) | copy-start | bytes 100
  180.6 2.4 collective-permute-start.23
  181.1 2.6 collective-permute-start.24
  188.2 40.7 %all-to-all-start.2 = ((bf16[32,320,128]{2,1,0:T(8,128)(2,1)}), bf16[32,320,128]{2,1,0:T(8,128)(2,1)}, u32[]{:S(2)}, u32[]{:S(2)}) async-start(bf16[32,320,128]{2,1,0:T(8,128)(2,1)} %branch_2_fun.1), calls=%async_computation.2 | async-start | bytes 5242880 | tf_op jit(solution)/shard_map/cond/branch_2_fun/all_to_all | solution.py:383
  242.2 21.1 %all-to-all-start.6 = ((f32[32,40,128]{2,1,0:T(8,128)}), f32[32,40,128]{2,1,0:T(8,128)S(1)}, u32[]{:S(2)}, u32[]{:S(2)}) async-start(f32[32,40,128]{2,1,0:T(8,128)} %get-tuple-element.449), calls=%async_computation.6 | async-start | bytes 1310720 | tf_op jit(solution)/shard_map/all_to_all | solution.py:383
  (5 other events, 27.0 us)
